TPU v7x, 256 devices: a whole 4x4x8 slice. The times are simulated.
256 devices in a mesh: band: 64 (over z, y, core), lev: 4 (over x).
Axes of the slice: x: 4, y: 4, z: 8, core: 2. Of those that a mesh axis runs over, the one named last changes fastest.
Arguments:
- grid_adjoint: float32 [1024, 64, 2048], P('band', 'lev'), may hold values from -6 to 6
- trajectory: float32 [1024, 64, 2048], P('band', 'lev'), may hold values from -3 to 3
- legendre_north: float32 [512, 512, 512], P(('band', 'lev')), may hold values from -0.25 to 0.25
- slot_wavenumber: int32 [512], replicated, may hold values from 0 to 511, each once
- spectral_state: float32 [512, 512, 2, 64], P(('band', 'lev')), may hold values from -6 to 6
- to_modes: float32 [64, 64], replicated, may hold values from -0.75 to 0.75
- from_modes: float32 [64, 64], replicated, may hold values from -0.75 to 0.75
- rates: float32 [64], replicated, may hold values from 0.1 to 10
Outputs:
- spectral_out: float32 [512, 512, 2, 64], P(('band', 'lev'))
- grid_out: float32 [1024, 64, 2048], P('band', 'lev')
Inputs may be any that keep to these rules, and one draw needn't show every extreme that they name: `slot_wavenumber`: each wavenumber stands in exactly one slot.
All inputs are finite; a program needn't handle non-finite values.
Results may differ from a plain program's by a relative error of at most 0.000067.
Values sent between devices are 32-bit elements; how exact they have to be, the bound alone decides.
No kernel may reach another device: no remote copies, remote signals or barrier semaphores. Data moves between devices by JAX's collectives and lax.ppermute only.
A program may use at most 128 MiB of HBM per device.

v0:
```python
import jax
import jax.numpy as jnp
import numpy as np
from jax import lax
from jax.experimental import pallas as pl
from jax.experimental.pallas import tpu as pltpu
from jax.sharding import PartitionSpec as P

WAVES = 512
LON = 2048
QUARTER = LON // 4
RESIDUES = (0, 2, 1, 3)
BF16 = jnp.bfloat16
F32 = jnp.float32


def wave_rows():
    j = np.arange(QUARTER, dtype=np.int64)
    blocks = []
    for residue in RESIDUES:
        m = 4 * np.arange(WAVES // 4, dtype=np.int64) + residue
        angle = (m[:, None] * j[None, :] % LON) * (2.0 * np.pi / LON)
        blocks += [np.cos(angle), -np.sin(angle)]
    table = (np.concatenate(blocks, axis=0) * LON**-0.5).astype(np.float32)
    high = table.astype(jnp.bfloat16)
    low = (table - high.astype(np.float32)).astype(jnp.bfloat16)
    return high, low


def split(value):
    high = value.astype(BF16)
    low = (value - high.astype(F32)).astype(BF16)
    return high, low


def mm(a, b):
    return lax.dot_general(a, b, (((1,), (0,)), ((), ())), preferred_element_type=F32)


def mm_nt(a, b):
    return lax.dot_general(a, b, (((1,), (1,)), ((), ())), preferred_element_type=F32)


def mm3(a, b):
    return mm(a[0], b[0]) + (mm(a[0], b[1]) + mm(a[1], b[0]))


def mm3_nt(a, b):
    return mm_nt(a[0], b[0]) + (mm_nt(a[0], b[1]) + mm_nt(a[1], b[0]))


def one_hot(slots_row):
    held = jnp.transpose(jnp.broadcast_to(slots_row.astype(F32), (128, WAVES)))
    lane = lax.broadcasted_iota(jnp.int32, (WAVES, 128), 1).astype(F32) * 4.0
    return jnp.concatenate(
        [(held == lane + float(r)).astype(F32).astype(BF16) for r in RESIDUES], axis=1
    )


def head_kernel(slots_ref, grid_ref, traj_ref, high_ref, low_ref, out_ref, work):
    half = QUARTER // 2
    for i in range(16):
        forced = grid_ref[i] * (1.0 + traj_ref[i])
        q0, q1, q2, q3 = (forced[:, QUARTER * q : QUARTER * (q + 1)] for q in range(4))
        even, swing = q0 + q2, q1 + q3
        rows = pl.ds(i, 16, stride=16)
        for n, part in enumerate((even + swing, even - swing, q0 - q2, q1 - q3)):
            for t in range(2 * half // 128):
                work[n, t, rows, :] = part[:, 128 * t : 128 * (t + 1)]
    full = lambda n: split(jnp.concatenate([work[n, t] for t in range(4)], axis=1))
    table = lambda a, b: (high_ref[a:b, :], low_ref[a:b, :])
    zero = mm3_nt(table(0, 256), full(0))
    two = mm3_nt(table(256, 512), full(1))
    odd = table(512, 1024)
    u1 = mm3_nt(odd, full(2))
    u2 = mm3_nt(odd, full(3))
    cosine = [zero[:128], two[:128], u1[:128] + u2[128:256], u1[256:384] - u2[384:]]
    sine = [zero[128:], two[128:], u1[128:256] - u2[:128], u1[384:] + u2[256:384]]
    pick = one_hot(slots_ref[...])
    for c, parts in enumerate((cosine, sine)):
        h, l = split(jnp.concatenate(parts, axis=0))
        slotted = mm(pick, h) + mm(pick, l)
        for k in range(2):
            out_ref[pl.ds(2 * k + c, WAVES, stride=4), :] = slotted[:, 128 * k : 128 * (k + 1)]


def prepare_kernel(slots_ref, p_ref, km_ref, kf_ref, ph_ref, pl_ref, th_ref, tl_ref, kh_ref, kl_ref, pick_ref):
    for s in range(2):
        value = p_ref[s]
        ph_ref[s], pl_ref[s] = split(value)
        th_ref[s], tl_ref[s] = split(jnp.transpose(value))
    kh_ref[0], kl_ref[0] = split(km_ref[...])
    kh_ref[1], kl_ref[1] = split(kf_ref[...])
    pick_ref[...] = one_hot(slots_ref[...])


def swap_groups(tiles, group):
    tiles = list(tiles)
    for bit in (1, 2, 4):
        mask = (group & bit) != 0
        for i in range(8):
            if i & bit:
                continue
            a, b = tiles[i], tiles[i | bit]
            tiles[i] = jnp.where(mask, pltpu.roll(b, 16 * bit, 1), a)
            tiles[i | bit] = jnp.where(mask, b, pltpu.roll(a, 128 - 16 * bit, 1))
    return tiles


def blocks_of(l_dim):
    return [(h * 64 + c * 32 + v * 8, c * 64 + v * 16 + h * 8) for c in range(2) for v in range(4) for h in range(2)]


def mid_kernel(
    waves_ref, y_ref, ph_ref, pl_ref, th_ref, tl_ref, kh_ref, kl_ref, scale_ref, state_ref,
    spectral_ref, z_ref, work,
):
    lane = lax.broadcasted_iota(jnp.int32, (8, 128), 1)
    group = lane // 16
    mirror = lane + 15 - 2 * (lane % 16)
    flip = lambda tile: jnp.take_along_axis(tile, mirror, axis=1)
    for v in range(4):
        for g in range(4):
            north = [y_ref[(8 * g + i) * 4 + v] for i in range(8)]
            south = [flip(y_ref[(63 - 8 * g - i) * 4 + v]) for i in range(8)]
            for par in range(2):
                folded = [n + s if par == 0 else n - s for n, s in zip(north, south)]
                for j, tile in enumerate(swap_groups(folded, group)):
                    work[par, g, pl.ds(v * 8 + j, 8, stride=32), :] = tile
    k_row = lax.broadcasted_iota(jnp.int32, (1, WAVES), 1)
    even_k = k_row % 2 == 0
    totals = []
    for s in range(2):
        rows = pl.ds(128 * s, 128)
        fold = [jnp.concatenate([work[par, g, rows, :] for g in range(4)], axis=1) for par in range(2)]
        both = mm3(split(jnp.concatenate(fold, axis=0)), (th_ref[s], tl_ref[s]))
        mixed = jnp.where(even_k, both[:128], both[128:])
        mixed = jnp.concatenate([mixed[a : a + 8] for a, _ in blocks_of(64)], axis=0)
        valid = (k_row < WAVES - waves_ref[s]).astype(F32)
        totals.append((mixed + state_ref[128 * s : 128 * (s + 1), :]) * valid)
    modes = mm3((kh_ref[0], kl_ref[0]), split(jnp.concatenate(totals, axis=0)))
    scales = [scale_ref[s] for s in (0, 0, 1, 1)]
    scaled = modes * jnp.concatenate(scales, axis=0)
    spectral = mm3((kh_ref[1], kl_ref[1]), split(scaled))
    spectral_ref[...] = spectral
    for s in range(2):
        own = spectral[128 * s : 128 * (s + 1)]
        pair = jnp.concatenate([jnp.where(even_k, own, 0.0), jnp.where(even_k, 0.0, own)], axis=0)
        both = mm3(split(pair), (ph_ref[s], pl_ref[s]))
        for par, side in enumerate((both[:128] + both[128:], both[:128] - both[128:])):
            for to, start in blocks_of(64):
                for g in range(4):
                    work[par, g, 128 * s + to : 128 * s + to + 8, :] = side[start : start + 8, 128 * g : 128 * (g + 1)]
    for v in range(4):
        for g in range(4):
            for par in range(2):
                tiles = [work[par, g, pl.ds(v * 8 + j, 8, stride=32), :] for j in range(8)]
                for i, tile in enumerate(swap_groups(tiles, group)):
                    if par == 0:
                        z_ref[(8 * g + i) * 4 + v] = tile
                    else:
                        z_ref[(63 - 8 * g - i) * 4 + v] = flip(tile)


def tail_kernel(z_ref, pick_ref, high_ref, low_ref, out_ref, work):
    pick = pick_ref[...]
    natural = []
    for c in range(2):
        sides = [z_ref[pl.ds(2 * k + c, WAVES, stride=4), :] for k in range(2)]
        h, l = split(jnp.transpose(jnp.concatenate(sides, axis=1)))
        natural.append(split(mm(h, pick) + mm(l, pick)))
    part = lambda c, kind: tuple(natural[c][n][:, 128 * kind : 128 * (kind + 1)] for n in range(2))
    minus = lambda pair: (-pair[0], -pair[1])
    join = lambda *parts: tuple(jnp.concatenate([p[n] for p in parts], axis=1) for n in range(2))
    table = lambda a, b: (high_ref[a:b, :], low_ref[a:b, :])
    zero = mm3(join(part(0, 0), part(1, 0)), table(0, 256))
    two = mm3(join(part(0, 1), part(1, 1)), table(256, 512))
    odd = table(512, 1024)
    first = mm3(join(part(0, 2), part(1, 2), part(0, 3), part(1, 3)), odd)
    turned = mm3(join(minus(part(1, 2)), part(0, 2), part(1, 3), minus(part(0, 3))), odd)
    plus, less = zero + two, zero - two
    for q, value in enumerate((plus + first, less + turned, plus - first, less - turned)):
        for t in range(4):
            work[4 * q + t] = value[:, 128 * t : 128 * (t + 1)]
    for t in range(16):
        for i in range(16):
            out_ref[i, :, 128 * t : 128 * (t + 1)] = work[t, pl.ds(i, 16, stride=16), :]


VMEM = pl.BlockSpec(memory_space=pltpu.VMEM)
SMEM = pl.BlockSpec(memory_space=pltpu.SMEM)


def call(kernel, name, outs, in_specs, scratch=(), flops=0, moved=0):
    return pl.pallas_call(
        kernel,
        name=name,
        out_shape=outs,
        in_specs=in_specs,
        out_specs=jax.tree.map(lambda _: VMEM, outs),
        scratch_shapes=list(scratch),
        compiler_params=pltpu.CompilerParams(vmem_limit_bytes=48 * 2**20),
        cost_estimate=pl.CostEstimate(flops=flops, bytes_accessed=moved, transcendentals=0),
    )


def shards(grid_adjoint, trajectory, legendre_north, slot_wavenumber, spectral_state, to_modes, from_modes, rates):
    shape = jax.ShapeDtypeStruct
    high, low = wave_rows()
    high, low = jnp.asarray(high), jnp.asarray(low)
    slots_row = slot_wavenumber.reshape(1, WAVES)
    device = lax.axis_index("band") * lax.axis_size("lev") + lax.axis_index("lev")
    own_waves = lax.dynamic_slice_in_dim(slot_wavenumber, 2 * device, 2)

    sent = call(
        head_kernel, "head", shape((2048, 128), F32), [VMEM] * 5,
        [pltpu.VMEM((4, 4, 256, 128), F32)], flops=2 * 10**9, moved=7 * 10**6,
    )(slots_row, grid_adjoint, trajectory, high, low)
    arrived = lax.all_to_all(sent.reshape(256, 8, 128), ("band", "lev"), 0, 0, tiled=True)

    k = jnp.arange(WAVES, dtype=jnp.int32)
    degree = (own_waves[:, None] + k[None, :]).astype(F32)
    helm = degree * (degree + 1.0) / (WAVES * (WAVES - 1.0))
    scale = 1.0 / (1.0 + helm[:, None, :] * rates[None, :, None])
    diagonal = jnp.eye(4, dtype=F32)
    outs = [shape((2, 512, 512), BF16)] * 4 + [shape((2, 256, 256), BF16)] * 2 + [shape((512, 512), BF16)]
    ph, plo, th, tl, kh, kl, pick = call(
        prepare_kernel, "prepare", outs, [VMEM] * 4, flops=10**8, moved=8 * 10**6
    )(slots_row, legendre_north, jnp.kron(diagonal, to_modes), jnp.kron(diagonal, from_modes))
    state = jnp.transpose(spectral_state, (0, 2, 3, 1)).reshape(256, WAVES)

    spectral, back = call(
        mid_kernel, "mid", [shape((256, WAVES), F32), shape((256, 8, 128), F32)], [SMEM] + [VMEM] * 9,
        [pltpu.VMEM((2, 4, 256, 128), F32)], flops=3 * 10**9, moved=8 * 10**6,
    )(own_waves, arrived, ph, plo, th, tl, kh, kl, scale, state)
    returned = lax.all_to_all(back, ("band", "lev"), 0, 0, tiled=True)
    grid = call(
        tail_kernel, "tail", shape((16, 16, LON), F32), [VMEM] * 4,
        [pltpu.VMEM((16, 256, 128), F32)], flops=2 * 10**9, moved=6 * 10**6,
    )(returned.reshape(2048, 128), pick, high, low)
    spectral_out = jnp.transpose(spectral.reshape(2, 2, 64, WAVES), (0, 3, 1, 2))
    return spectral_out, grid


def solution(mesh):
    spread = P(("band", "lev"), None, None)
    return jax.shard_map(
        shards,
        mesh=mesh,
        in_specs=(
            P("band", "lev", None), P("band", "lev", None), spread, P(),
            P(("band", "lev"), None, None, None), P(), P(), P(),
        ),
        out_specs=(P(("band", "lev"), None, None, None), P("band", "lev", None)),
        check_vma=False,
    )
```

profile of v0, /device:TPU:1, one launch (start us, length us, event | category | flops | bytes accessed | tf_op | source)
XLA Modules:
  0.0 109.4 jit_solution(11198460818782181540)
XLA Ops:
  0.6 0.0 copy-start
  0.6 0.7 copy-done
  1.3 1.6 %copy-done.2 = f32[16,16,2048]{2,1,0:T(8,128)S(1)} copy-done((f32[16,16,2048]{2,1,0:T(8,128)S(1)}, f32[16,16,2048]{2,1,0:T(8,128)}, u32[]{:S(2)}) %copy-start.2) | copy-done | bytes 2097176
  2.9 1.2 %copy-done.12 = bf16[1024,512]{1,0:T(8,128)(2,1)S(1)} copy-done((bf16[1024,512]{1,0:T(8,128)(2,1)S(1)}, bf16[1024,512]{1,0:T(8,128)(2,1)}, u32[]{:S(2)}) %copy-start.12) | copy-done | bytes 1048600
  4.1 1.2 %copy-done.14 = bf16[1024,512]{1,0:T(8,128)(2,1)S(1)} copy-done((bf16[1024,512]{1,0:T(8,128)(2,1)S(1)}, bf16[1024,512]{1,0:T(8,128)(2,1)}, u32[]{:S(2)}) %copy-start.14) | copy-done | bytes 1048600
  5.4 6.6 %head.1 = f32[2048,128]{1,0:T(8,128)} custom-call(s32[1,512]{1,0:T(1,128)S(1)} %bitcast.10, f32[16,16,2048]{2,1,0:T(8,128)S(1)} %copy-done.2, f32[16,16,2048]{2,1,0:T(8,128)} %traj_ref.1, bf16[1024,512]{1,0:T(8,128)(2,1)S(1)} %copy-done.14, bf16[1024,512]{1,0:T(8,128)(2,1)S(1)} %copy-done.12), custom_call_target="tpu_custom_call" | custom-call | flops 2000000000 | bytes 7000000 | tf_op jit(solution)/shard_map/head/pallas_call | solution.py:215
  11.9 15.7 %all-to-all-start = ((f32[256,8,128]{2,1,0:T(8,128)}), f32[256,8,128]{2,1,0:T(8,128)S(1)}, u32[]{:S(2)}, u32[]{:S(2)}) async-start(f32[256,8,128]{2,1,0:T(8,128)} %bitcast.1), calls=%async_computation | async-start | bytes 2097152 | tf_op jit(solution)/shard_map/all_to_all | solution.py:219
  27.6 0.0 copy-done.1
  27.6 0.1 dynamic_slice.3.waves_ref
  27.7 0.0 copy-done.16
  27.7 0.0 copy-done.17
  27.7 0.2 broadcast_multiply_fusion
  27.9 0.0 copy-start.18
  27.9 0.0 copy-start.7
  27.9 0.3 mul.71.kf_ref
  28.3 0.3 mul.68.km_ref
  28.6 2.4 %prepare.1 = (bf16[2,512,512]{2,1,0:T(8,128)(2,1)S(1)}, bf16[2,512,512]{2,1,0:T(8,128)(2,1)S(1)}, bf16[2,512,512]{2,1,0:T(8,128)(2,1)S(1)}, bf16[2,512,512]{2,1,...) custom-call(s32[1,512]{1,0:T(1,128)S(1)} %bitcast.11, ...), custom_call_target="tpu_custom_call" | custom-call | flops 100000000 | bytes 8000000 | tf_op jit(solution)/shard_map/prepare/pallas_call | solution.py:227
  31.0 0.0 copy-start.3
  31.0 1.0 copy-done.3
  32.0 1.0 copy-done.5
  33.0 1.0 copy-done.6
  34.0 0.8 copy-done.8
  34.7 0.7 copy-done.10
  35.4 0.1 fusion
  35.5 0.0 copy-done.18
  35.5 0.1 add_divide_fusion.scale_ref
  35.6 22.9 %all-to-all-done.y_ref = f32[256,8,128]{2,1,0:T(8,128)S(1)} async-done(((f32[256,8,128]{2,1,0:T(8,128)}), f32[256,8,128]{2,1,0:T(8,128)S(1)}, u32[]{:S(2)}, u32[]{:S(2)}) %all-to-all-start) | async-done | bytes 1048608 | tf_op jit(solution)/shard_map/all_to_all | solution.py:219
  58.5 1.2 %copy-done.4 = bf16[2,512,512]{2,1,0:T(8,128)(2,1)S(1)} copy-done((bf16[2,512,512]{2,1,0:T(8,128)(2,1)S(1)}, bf16[2,512,512]{2,1,0:T(8,128)(2,1)}, u32[]{:S(2)}) %copy-start.4) | copy-done | bytes 1048600
  59.8 0.9 copy-done.11
  60.7 7.3 %mid.1 = (f32[256,512]{1,0:T(8,128)}, f32[256,8,128]{2,1,0:T(8,128)S(1)}) custom-call(s32[2]{0:T(128)S(1)} %dynamic_slice.3.waves_ref, f32[256,8,128]{2,1,0:T(8,128)S(1)} %all-to-all-done.y_ref, bf16[2,512,512]{2,1,0:T(8,128)(2,1)S(1)} %get-tuple-element.11.ph_ref, bf16[2,512,512]{2,1,0:T(8,128)(2,1)S(1)} %copy-done.4, bf16[2,512,512]{2,1,0:T(8,128)(2,1)} %copy-done.5, ...), custom_call_target="tpu_custom_call" | custom-call | flops 3000000000 | bytes 8000000 | tf_op jit(solution)/shard_map/mid/pallas_call | solution.py:232
  68.0 37.3 %all_to_all.10 = f32[256,8,128]{2,1,0:T(8,128)S(1)} all-to-all(f32[256,8,128]{2,1,0:T(8,128)S(1)} %get-tuple-element.18), channel_id=1, replica_groups=mesh['band'=64,'lev'=4] {'band','lev'}, dimensions={0} | all-to-all | bytes 2097152 | tf_op jit(solution)/shard_map/all_to_all | solution.py:236
  105.4 4.0 %tail.1 = f32[16,16,2048]{2,1,0:T(8,128)} custom-call(f32[2048,128]{1,0:T(8,128)S(1)} %bitcast.9, bf16[512,512]{1,0:T(8,128)(2,1)S(1)} %copy-done.9, bf16[1024,512]{1,0:T(8,128)(2,1)S(1)} %copy-done.15, bf16[1024,512]{1,0:T(8,128)(2,1)S(1)} %copy-done.13), custom_call_target="tpu_custom_call" | custom-call | flops 2000000000 | bytes 6000000 | tf_op jit(solution)/shard_map/tail/pallas_call | solution.py:237
  (20 shorter events, 0.0 us)
Async XLA Ops:
  0.6 0.7 copy-start
  1.3 1.6 %copy-start.2 = (f32[16,16,2048]{2,1,0:T(8,128)S(1)}, f32[16,16,2048]{2,1,0:T(8,128)}, u32[]{:S(2)}) copy-start(f32[16,16,2048]{2,1,0:T(8,128)} %grid_ref.1) | copy-start | bytes 6291460
  2.9 1.2 %copy-start.12 = (bf16[1024,512]{1,0:T(8,128)(2,1)S(1)}, bf16[1024,512]{1,0:T(8,128)(2,1)}, u32[]{:S(2)}) copy-start(bf16[1024,512]{1,0:T(8,128)(2,1)} %constant.28.clone.low_ref) | copy-start | bytes 3145732
  4.1 1.2 %copy-start.14 = (bf16[1024,512]{1,0:T(8,128)(2,1)S(1)}, bf16[1024,512]{1,0:T(8,128)(2,1)}, u32[]{:S(2)}) copy-start(bf16[1024,512]{1,0:T(8,128)(2,1)} %constant.27.clone.high_ref) | copy-start | bytes 3145732
  11.9 15.7 %copy-start.1 = (s32[512]{0:T(512)S(1)}, s32[512]{0:T(512)}, u32[]{:S(2)}) copy-start(s32[512]{0:T(512)} %param.13) | copy-start | bytes 6148
  11.9 15.8 %copy-start.16 = (f32[64,64]{1,0:T(8,128)S(1)}, f32[64,64]{1,0:T(8,128)}, u32[]{:S(2)}) copy-start(f32[64,64]{1,0:T(8,128)} %param.16) | copy-start | bytes 49156
  11.9 15.8 %copy-start.17 = (f32[64,64]{1,0:T(8,128)S(1)}, f32[64,64]{1,0:T(8,128)}, u32[]{:S(2)}) copy-start(f32[64,64]{1,0:T(8,128)} %param.15) | copy-start | bytes 49156
  11.9 46.6 %all-to-all-start = ((f32[256,8,128]{2,1,0:T(8,128)}), f32[256,8,128]{2,1,0:T(8,128)S(1)}, u32[]{:S(2)}, u32[]{:S(2)}) async-start(f32[256,8,128]{2,1,0:T(8,128)} %bitcast.1), calls=%async_computation | async-start | bytes 2097152 | tf_op jit(solution)/shard_map/all_to_all | solution.py:219
  27.9 7.6 %copy-start.18 = (f32[64]{0:T(128)S(1)}, f32[64]{0:T(128)}, u32[]{:S(2)}) copy-start(f32[64]{0:T(128)} %param.17) | copy-start | bytes 772
  27.9 30.6 %copy-start.7 = (f32[2,512,2,64]{1,3,2,0:T(8,128)S(1)}, f32[2,512,2,64]{1,3,2,0:T(8,128)}, u32[]{:S(2)}) copy-start(f32[2,512,2,64]{1,3,2,0:T(8,128)} %param.14) | copy-start | bytes 1572868
  31.0 1.0 copy-start.3
  32.0 1.0 copy-start.5
  33.0 1.0 copy-start.6
  34.0 0.8 copy-start.8
  34.7 0.7 copy-start.10
  58.5 1.2 %copy-start.4 = (bf16[2,512,512]{2,1,0:T(8,128)(2,1)S(1)}, bf16[2,512,512]{2,1,0:T(8,128)(2,1)}, u32[]{:S(2)}) copy-start(bf16[2,512,512]{2,1,0:T(8,128)(2,1)} %copy-done.3) | copy-start | bytes 3145732
  59.7 0.9 copy-start.11
  60.7 44.7 %copy-start.15 = (bf16[1024,512]{1,0:T(8,128)(2,1)S(1)}, bf16[1024,512]{1,0:T(8,128)(2,1)}, u32[]{:S(2)}) copy-start(bf16[1024,512]{1,0:T(8,128)(2,1)} %constant.27.clone.high_ref) | copy-start | bytes 3145732
  68.0 37.3 %copy-start.9 = (bf16[512,512]{1,0:T(8,128)(2,1)S(1)}, bf16[512,512]{1,0:T(8,128)(2,1)}, u32[]{:S(2)}) copy-start(bf16[512,512]{1,0:T(8,128)(2,1)} %copy-done.8) | copy-start | bytes 1572868
  68.0 37.3 %copy-start.13 = (bf16[1024,512]{1,0:T(8,128)(2,1)S(1)}, bf16[1024,512]{1,0:T(8,128)(2,1)}, u32[]{:S(2)}) copy-start(bf16[1024,512]{1,0:T(8,128)(2,1)} %constant.28.clone.low_ref) | copy-start | bytes 3145732
where the time goes:
time: 110 us; the launch traced here: 109 us
  blocking collectives  37.3 us (34%)
  waiting for transfers between devices  22.9 us (21%)
  Pallas kernels  20.3 us (18%)
  starting transfers between devices  15.7 us (14%)
  local copies, waits for them, and re-layouts  12.1 us (11%)
    all_to_all x1, blocking collectives, shards(): returned = lax.all_to_all(back, ('band', 'lev'), 0, 0, tiled=True)  37.3 us
    all_to_all x1, waiting for transfers between devices, shards(): lax.all_to_all(sent.reshape(256, 8, 128), ('band', 'lev'), 0, 0, tiled=True)  22.9 us
    all_to_all x1, starting transfers between devices, shards(): lax.all_to_all(sent.reshape(256, 8, 128), ('band', 'lev'), 0, 0, tiled=True)  15.7 us
    unnamed x38, local copies, waits for them, and re-layouts  11.3 us
    pallas_call x1, Pallas kernels, shards(): call(mid_kernel, 'mid', [shape((256, WAVES), F32), shape((256, 8, 128), F...  7.33 us
    pallas_call x1, Pallas kernels, shards(): call(head_kernel, 'head', shape((2048, 128), F32), [VMEM] * 5, [pltpu.VME...  6.55 us
    pallas_call x1, Pallas kernels, shards(): call(tail_kernel, 'tail', shape((16, 16, LON), F32), [VMEM] * 4, [pltpu.V...  4.02 us
    pallas_call x1, Pallas kernels, shards(): call(prepare_kernel, 'prepare', outs, [VMEM] * 4, flops=10 ** 8, moved=8...  2.39 us
  transfers between devices with their start and end apart: 1, of which 1 were waited for; matrix products, arithmetic and copies ran while one was open for 1% of the time, Pallas kernels for 2%

commit v1 on v0

v1 whole, which is shorter than its diff:
```python
import jax
import jax.numpy as jnp
import numpy as np
from jax import lax
from jax.experimental import pallas as pl
from jax.experimental.pallas import tpu as pltpu
from jax.sharding import PartitionSpec as P

WAVES = 512
LON = 2048
QUARTER = LON // 4
RESIDUES = (0, 2, 1, 3)
BF16 = jnp.bfloat16
F32 = jnp.float32


def wave_rows():
    j = np.arange(QUARTER, dtype=np.int64)
    blocks = []
    for residue in RESIDUES:
        m = 4 * np.arange(WAVES // 4, dtype=np.int64) + residue
        angle = (m[:, None] * j[None, :] % LON) * (2.0 * np.pi / LON)
        blocks += [np.cos(angle), -np.sin(angle)]
    table = (np.concatenate(blocks, axis=0) * LON**-0.5).astype(np.float32)
    high = table.astype(jnp.bfloat16)
    low = (table - high.astype(np.float32)).astype(jnp.bfloat16)
    return high, low


def split(value):
    high = value.astype(BF16)
    low = (value - high.astype(F32)).astype(BF16)
    return high, low


def mm(a, b):
    return lax.dot_general(a, b, (((1,), (0,)), ((), ())), preferred_element_type=F32)


def mm_nt(a, b):
    return lax.dot_general(a, b, (((1,), (1,)), ((), ())), preferred_element_type=F32)


def mm3(a, b):
    return mm(a[0], b[0]) + (mm(a[0], b[1]) + mm(a[1], b[0]))


def mm3_nt(a, b):
    return mm_nt(a[0], b[0]) + (mm_nt(a[0], b[1]) + mm_nt(a[1], b[0]))


def one_hot(slots_row):
    held = jnp.transpose(jnp.broadcast_to(slots_row.astype(F32), (128, WAVES)))
    lane = lax.broadcasted_iota(jnp.int32, (WAVES, 128), 1).astype(F32) * 4.0
    return jnp.concatenate(
        [(held == lane + float(r)).astype(F32).astype(BF16) for r in RESIDUES], axis=1
    )


def head_kernel(
    slots_ref, grid_hbm, traj_hbm, high_hbm, low_hbm, out_hbm,
    grid_ref, traj_ref, high_ref, low_ref, parts, sent, sems,
):
    copies = []
    for t in range(16):
        columns = pl.ds(128 * (4 * (t % 4) + t // 4), 128)
        for k, (src, dst) in enumerate(((grid_hbm, grid_ref), (traj_hbm, traj_ref))):
            copies.append(pltpu.make_async_copy(src.at[:, columns], dst.at[t], sems.at[2 * t + k]))
    tables = [
        pltpu.make_async_copy(src, dst, sems.at[32 + k])
        for k, (src, dst) in enumerate(((high_hbm, high_ref), (low_hbm, low_ref)))
    ]
    for copy in copies + tables:
        copy.start()
    pick = one_hot(slots_ref[...])
    for t in range(4):
        for copy in copies[8 * t : 8 * t + 8]:
            copy.wait()
        lanes = pl.ds(128 * t, 128)
        for level in range(16):
            lats = pl.ds(level, 16, stride=16)
            q0, q1, q2, q3 = (
                grid_ref[4 * t + q, lats, :] * (1.0 + traj_ref[4 * t + q, lats, :]) for q in range(4)
            )
            even, swing = q0 + q2, q1 + q3
            rows = pl.ds(16 * level, 16)
            for n, part in enumerate((even + swing, even - swing, q0 - q2, q1 - q3)):
                parts[n, 0, rows, lanes], parts[n, 1, rows, lanes] = split(part)
    for copy in tables:
        copy.wait()

    def product(a, b, n):
        count = b - a
        both = jnp.concatenate([high_ref[a:b, :], low_ref[a:b, :]], axis=0)
        wide = mm_nt(both, parts[n, 0])
        return wide[:count] + wide[count:] + mm_nt(high_ref[a:b, :], parts[n, 1])

    zero, two, u1, u2 = product(0, 256, 0), product(256, 512, 1), product(512, 1024, 2), product(512, 1024, 3)
    cosine = [zero[:128], two[:128], u1[:128] + u2[128:256], u1[256:384] - u2[384:]]
    sine = [zero[128:], two[128:], u1[128:256] - u2[:128], u1[384:] + u2[256:384]]
    sides = [split(jnp.concatenate(wave, axis=0)) for wave in (cosine, sine)]
    wide = jnp.concatenate([sides[0][0], sides[1][0], sides[0][1], sides[1][1]], axis=1)
    stores = []
    for n in range(4):
        found = mm(pick[128 * n : 128 * (n + 1)], wide)
        found = found[:, :512] + found[:, 512:]
        for c in range(2):
            for k in range(2):
                sent[pl.ds(512 * n + 2 * k + c, 128, stride=4), :] = found[:, 256 * c + 128 * k : 256 * c + 128 * (k + 1)]
        rows = pl.ds(512 * n, 512)
        stores.append(pltpu.make_async_copy(sent.at[rows], out_hbm.at[rows], sems.at[34 + n]))
        stores[-1].start()
    for copy in stores:
        copy.wait()


def prepare_kernel(slots_ref, p_ref, high_ref, low_ref, pick_ref):
    for s in range(2):
        high_ref[s], low_ref[s] = split(p_ref[s])
    pick_ref[...] = one_hot(slots_ref[...])


def swap_groups(tiles, group):
    tiles = list(tiles)
    for bit in (1, 2, 4):
        mask = (group & bit) != 0
        for i in range(8):
            if i & bit:
                continue
            a, b = tiles[i], tiles[i | bit]
            tiles[i] = jnp.where(mask, pltpu.roll(b, 16 * bit, 1), a)
            tiles[i | bit] = jnp.where(mask, b, pltpu.roll(a, 128 - 16 * bit, 1))
    return tiles


def mid_kernel(
    waves_ref, rates_ref, to_ref, from_ref, y_ref, ph_hbm, pl_hbm, state_hbm,
    spectral_hbm, z_ref,
    ph_ref, pl_ref, state_ref, spectral_ref, folds, north, south, sems,
):
    sources, targets = (ph_hbm, pl_hbm, state_hbm), (ph_ref, pl_ref, state_ref)
    copies = [pltpu.make_async_copy(a, b, sems.at[k]) for k, (a, b) in enumerate(zip(sources, targets))]
    for copy in copies:
        copy.start()
    lane = lax.broadcasted_iota(jnp.int32, (8, 128), 1)
    group = lane // 16
    mirror = lane + 15 - 2 * (lane % 16)
    flip = lambda tile: jnp.take_along_axis(tile, mirror, axis=1)

    def fold_step(step, carry):
        v, g = step // 4, step % 4
        ahead = swap_groups([y_ref[(8 * g + i) * 4 + v] for i in range(8)], group)
        behind = swap_groups([y_ref[(63 - 8 * g - i) * 4 + v] for i in range(8)], group)
        for j in range(8):
            a, b = ahead[j], flip(behind[j])
            rows = pl.ds(pl.multiple_of(64 * v + 8 * j, 8), 8)
            folds[0, g, rows, :] = a + b
            folds[1, g, rows, :] = a - b
        return carry

    lax.fori_loop(0, 16, fold_step, 0, unroll=4)
    k_row = lax.broadcasted_iota(jnp.int32, (1, WAVES), 1)
    even_k = k_row % 2 == 0
    to_modes, from_modes = split(to_ref[...]), split(from_ref[...])
    rate = jnp.broadcast_to(rates_ref[:, 0:1], (64, WAVES))
    for copy in copies:
        copy.wait()
    pick_rows = lambda pair, rows: tuple(p[rows] for p in pair)
    for s in range(2):
        fold = []
        for par in range(2):
            for c in range(2):
                halves = [
                    jnp.concatenate(
                        [folds[par, g, pl.ds(4 * s + 2 * h + c, 32, stride=8), :] for g in range(4)], axis=1
                    )
                    for h in range(2)
                ]
                fold += [halves[h][8 * v : 8 * v + 8] for v in range(4) for h in range(2)]
        both = mm3_nt(split(jnp.concatenate(fold, axis=0)), (ph_ref[s], pl_ref[s]))
        wave = waves_ref[s]
        valid = (k_row < WAVES - wave).astype(F32)
        degree = (k_row + wave).astype(F32)
        helm = degree * (degree + 1.0) / (WAVES * (WAVES - 1.0))
        scale = 1.0 / (1.0 + helm * rate)
        for c in range(2):
            rows = pl.ds(128 * s + 64 * c, 64)
            mixed = jnp.where(even_k, both[64 * c : 64 * c + 64], both[128 + 64 * c : 192 + 64 * c])
            total = (mixed + state_ref[rows, :]) * valid
            modes = mm3(to_modes, split(total)) * scale
            spectral_ref[rows, :] = mm3(from_modes, split(modes))
    store = pltpu.make_async_copy(spectral_ref, spectral_hbm, sems.at[3])
    store.start()
    for s in range(2):
        own = spectral_ref[128 * s : 128 * (s + 1), :]
        pair = jnp.concatenate([jnp.where(even_k, own, 0.0), jnp.where(even_k, 0.0, own)], axis=0)
        both = mm3(split(pair), (ph_ref[s], pl_ref[s]))
        for to, side in ((north, both[:128] + both[128:]), (south, both[:128] - both[128:])):
            for c in range(2):
                for v in range(4):
                    for h in range(2):
                        row, start = 128 * s + 64 * h + 32 * c + 8 * v, 64 * c + 16 * v + 8 * h
                        for g in range(4):
                            to[g, row : row + 8, :] = side[start : start + 8, 128 * g : 128 * (g + 1)]
    for v in range(4):
        for g in range(4):
            for side in (north, south):
                tiles = [side[g, pl.ds(v * 8 + j, 8, stride=32), :] for j in range(8)]
                for i, tile in enumerate(swap_groups(tiles, group)):
                    if side is north:
                        z_ref[(8 * g + i) * 4 + v] = tile
                    else:
                        z_ref[(63 - 8 * g - i) * 4 + v] = flip(tile)
    store.wait()


def tail_kernel(z_ref, pick_ref, high_ref, low_ref, out_hbm, work, block, sems):
    pick = pick_ref[...]
    natural = []
    for c in range(2):
        sides = [z_ref[pl.ds(2 * k + c, WAVES, stride=4), :] for k in range(2)]
        h, l = split(jnp.transpose(jnp.concatenate(sides, axis=1)))
        natural.append(split(mm(h, pick) + mm(l, pick)))
    part = lambda c, kind: tuple(natural[c][n][:, 128 * kind : 128 * (kind + 1)] for n in range(2))
    minus = lambda pair: (-pair[0], -pair[1])
    join = lambda *parts: tuple(jnp.concatenate([p[n] for p in parts], axis=1) for n in range(2))
    table = lambda a, b: (high_ref[a:b, :], low_ref[a:b, :])
    zero = mm3(join(part(0, 0), part(1, 0)), table(0, 256))
    two = mm3(join(part(0, 1), part(1, 1)), table(256, 512))
    odd = table(512, 1024)
    stores = []

    def put(q, value):
        for t in range(4):
            work[4 * q + t] = value[:, 128 * t : 128 * (t + 1)]
        for i in range(16):
            for t in range(4 * q, 4 * q + 4):
                block[i, :, 128 * t : 128 * (t + 1)] = work[t, pl.ds(i, 16, stride=16), :]
        columns = pl.ds(QUARTER * q, QUARTER)
        stores.append(pltpu.make_async_copy(block.at[:, :, columns], out_hbm.at[:, :, columns], sems.at[q]))
        stores[-1].start()

    plus, less = zero + two, zero - two
    first = mm3(join(part(0, 2), part(1, 2), part(0, 3), part(1, 3)), odd)
    put(0, plus + first)
    put(2, plus - first)
    turned = mm3(join(minus(part(1, 2)), part(0, 2), part(1, 3), minus(part(0, 3))), odd)
    put(1, less + turned)
    put(3, less - turned)
    for copy in stores:
        copy.wait()


VMEM = pl.BlockSpec(memory_space=pltpu.VMEM)
SMEM = pl.BlockSpec(memory_space=pltpu.SMEM)
HBM = pl.BlockSpec(memory_space=pltpu.HBM)
DMA = pltpu.SemaphoreType.DMA


def call(kernel, name, outs, in_specs, out_specs, scratch=(), flops=0, moved=0, room=32):
    return pl.pallas_call(
        kernel,
        name=name,
        out_shape=outs,
        in_specs=in_specs,
        out_specs=out_specs,
        scratch_shapes=list(scratch),
        compiler_params=pltpu.CompilerParams(vmem_limit_bytes=room * 2**20),
        cost_estimate=pl.CostEstimate(flops=flops, bytes_accessed=moved, transcendentals=0),
    )


def shards(grid_adjoint, trajectory, legendre_north, slot_wavenumber, spectral_state, to_modes, from_modes, rates):
    shape = jax.ShapeDtypeStruct
    high, low = wave_rows()
    high, low = jnp.asarray(high), jnp.asarray(low)
    slots_row = slot_wavenumber.reshape(1, WAVES)
    device = lax.axis_index("band") * lax.axis_size("lev") + lax.axis_index("lev")
    own_waves = lax.dynamic_slice_in_dim(slot_wavenumber, 2 * device, 2)

    square = (256, LON)
    sent = call(
        head_kernel, "head", shape((2048, 128), F32), [VMEM] + [HBM] * 4, HBM,
        [pltpu.VMEM((16, 256, 128), F32)] * 2 + [pltpu.VMEM((1024, QUARTER), BF16)] * 2
        + [pltpu.VMEM((4, 2, 256, QUARTER), BF16), pltpu.VMEM((2048, 128), F32), DMA((38,))],
        flops=2 * 10**9, moved=7 * 10**6, room=60,
    )(slots_row, grid_adjoint.reshape(square), trajectory.reshape(square), high, low)
    arrived = lax.all_to_all(sent.reshape(256, 8, 128), ("band", "lev"), 0, 0, tiled=True)

    ph, plo, pick = call(
        prepare_kernel, "prepare", [shape((2, 512, 512), BF16)] * 2 + [shape((512, 512), BF16)],
        [VMEM] * 2, [VMEM] * 3, flops=10**8, moved=8 * 10**6,
    )(slots_row, legendre_north)
    state = jnp.transpose(spectral_state, (0, 2, 3, 1)).reshape(256, WAVES)
    columns = jnp.broadcast_to(rates[:, None], (64, 128))
    far = [pltpu.with_memory_space_constraint(v, pltpu.HBM) for v in (ph, plo, state)]

    legendre, rows = pltpu.VMEM((2, 512, 512), BF16), pltpu.VMEM((256, WAVES), F32)
    spectral, back = call(
        mid_kernel, "mid", [shape((256, WAVES), F32), shape((256, 8, 128), F32)],
        [SMEM] + [VMEM] * 4 + [HBM] * 3, [HBM, VMEM],
        [legendre, legendre, rows, rows, pltpu.VMEM((2, 4, 256, 128), F32)]
        + [pltpu.VMEM((4, 256, 128), F32)] * 2 + [DMA((4,))],
        flops=3 * 10**9, moved=8 * 10**6, room=32,
    )(own_waves, columns, to_modes, from_modes, arrived, *far)
    returned = lax.all_to_all(back, ("band", "lev"), 0, 0, tiled=True)
    grid = call(
        tail_kernel, "tail", shape((16, 16, LON), F32), [VMEM] * 4, HBM,
        [pltpu.VMEM((16, 256, 128), F32), pltpu.VMEM((16, 16, LON), F32), DMA((4,))],
        flops=2 * 10**9, moved=6 * 10**6,
    )(returned.reshape(2048, 128), pick, high, low)
    spectral_out = jnp.transpose(spectral.reshape(2, 2, 64, WAVES), (0, 3, 1, 2))
    return spectral_out, grid


def solution(mesh):
    spread = P(("band", "lev"), None, None)
    return jax.shard_map(
        shards,
        mesh=mesh,
        in_specs=(
            P("band", "lev", None), P("band", "lev", None), spread, P(),
            P(("band", "lev"), None, None, None), P(), P(), P(),
        ),
        out_specs=(P(("band", "lev"), None, None, None), P("band", "lev", None)),
        check_vma=False,
    )
```

time: 110 us -> 104 us (0.945)
  local copies, waits for them, and re-layouts: 12.1 us -> 2.96 us
  waiting for transfers between devices: 22.9 us -> 27.3 us
    unnamed x38 -> x22, local copies, waits for them, and re-layouts: 11.3 us -> 2.82 us
    all_to_all x1, waiting for transfers between devices: 22.9 us -> 27.3 us  [shards(): lax.all_to_all(sent.reshape(256, 8, 128), ('band', 'lev'), 0, 0, tiled=True)]
  transfers between devices with their start and end apart: 1 -> 1, of which waited for: 1 -> 1; matrix products, arithmetic and copies ran while one was open for 1% -> 0% of each run, Pallas kernels for 2% -> 1%
where the time goes in v1:
time: 104 us
  blocking collectives  37.3 us (36%)
  waiting for transfers between devices  27.3 us (26%)
  Pallas kernels  19.6 us (19%)
  starting transfers between devices  15.7 us (15%)
  local copies, waits for them, and re-layouts  2.96 us (3%)
    all_to_all x1, blocking collectives, shards(): returned = lax.all_to_all(back, ('band', 'lev'), 0, 0, tiled=True)  37.3 us
    all_to_all x1, waiting for transfers between devices, shards(): lax.all_to_all(sent.reshape(256, 8, 128), ('band', 'lev'), 0, 0, tiled=True)  27.3 us
    all_to_all x1, starting transfers between devices, shards(): lax.all_to_all(sent.reshape(256, 8, 128), ('band', 'lev'), 0, 0, tiled=True)  15.7 us
    pallas_call x1, Pallas kernels, shards(): call(head_kernel, 'head', shape((2048, 128), F32), [VMEM] + [HBM] * 4, HB...  8.04 us
    pallas_call x1, Pallas kernels, shards(): call(mid_kernel, 'mid', [shape((256, WAVES), F32), shape((256, 8, 128), F...  7.1 us
    pallas_call x1, Pallas kernels, shards(): call(tail_kernel, 'tail', shape((16, 16, LON), F32), [VMEM] * 4, HBM, [pl...  3.71 us
    unnamed x22, local copies, waits for them, and re-layouts  2.82 us
  transfers between devices with their start and end apart: 1, of which 1 were waited for; matrix products, arithmetic and copies ran while one was open for 0% of the time, Pallas kernels for 1%

profile of v1, /device:TPU:1, one launch (start us, length us, event | category | flops | bytes accessed | tf_op | source)
XLA Modules:
  0.0 103.6 jit_solution(15411808881956567175)
XLA Ops:
  0.6 8.0 %head.1 = f32[2048,128]{1,0:T(8,128)} custom-call(s32[1,512]{1,0:T(1,128)} %bitcast.12, f32[256,2048]{1,0:T(8,128)} %bitcast.15, f32[256,2048]{1,0:T(8,128)} %bitcast.16, bf16[1024,512]{1,0:T(8,128)(2,1)} %constant.21.clone.high_hbm.high_ref, bf16[1024,512]{1,0:T(8,128)(2,1)} %constant.22.clone.low_hbm.low_ref), custom_call_target="tpu_custom_call" | custom-call | flops 2000000000 | bytes 7000000 | tf_op jit(solution)/shard_map/head/pallas_call | solution.py:282
  8.7 0.0 copy-start.1
  8.7 0.0 copy-start
  8.7 0.0 copy-start.10
  8.7 0.0 copy-start.6
  8.7 0.0 copy-start.7
  8.7 15.7 %all-to-all-start = ((f32[256,8,128]{2,1,0:T(8,128)}), f32[256,8,128]{2,1,0:T(8,128)S(1)}, u32[]{:S(2)}, u32[]{:S(2)}) async-start(f32[256,8,128]{2,1,0:T(8,128)} %bitcast.14), calls=%async_computation | async-start | bytes 2097152 | tf_op jit(solution)/shard_map/all_to_all | solution.py:288
  24.4 0.0 copy-done.1
  24.4 0.1 dynamic_slice.3.waves_ref
  24.5 0.0 copy-done
  24.5 0.7 prepare.1
  25.2 0.0 copy-start.2
  25.2 1.0 copy-done.2
  26.2 0.0 copy-start.3
  26.2 1.0 copy-done.3
  27.2 0.0 copy-start.4
  27.2 0.8 copy-done.4
  28.0 27.3 %all-to-all-done.y_ref = f32[256,8,128]{2,1,0:T(8,128)S(1)} async-done(((f32[256,8,128]{2,1,0:T(8,128)}), f32[256,8,128]{2,1,0:T(8,128)S(1)}, u32[]{:S(2)}, u32[]{:S(2)}) %all-to-all-start) | async-done | bytes 1048608 | tf_op jit(solution)/shard_map/all_to_all | solution.py:288
  55.4 0.0 copy-done.10
  55.4 0.1 broadcast_in_dim.2.rates_ref
  55.4 0.0 copy-done.6
  55.4 0.0 copy-done.7
  55.4 0.0 copy-start.9
  55.4 7.1 %mid.1 = (f32[256,512]{1,0:T(8,128)}, f32[256,8,128]{2,1,0:T(8,128)S(1)}) custom-call(s32[2]{0:T(128)S(1)} %dynamic_slice.3.waves_ref, f32[64,128]{1,0:T(8,128)S(1)} %broadcast_in_dim.2.rates_ref, f32[64,64]{1,0:T(8,128)S(1)} %copy-done.6, f32[64,64]{1,0:T(8,128)S(1)} %copy-done.7, f32[256,8,128]{2,1,0:T(8,128)S(1)} %all-to-all-done.y_ref, ...), custom_call_target="tpu_custom_call" | custom-call | flops 3000000000 | bytes 8000000 | tf_op jit(solution)/shard_map/mid/pallas_call | solution.py:299
  62.5 0.0 copy-start.5
  62.6 0.0 copy-start.8
  62.6 37.3 %all_to_all.10 = f32[256,8,128]{2,1,0:T(8,128)S(1)} all-to-all(f32[256,8,128]{2,1,0:T(8,128)S(1)} %get-tuple-element.10), channel_id=1, replica_groups=mesh['band'=64,'lev'=4] {'band','lev'}, dimensions={0} | all-to-all | bytes 2097152 | tf_op jit(solution)/shard_map/all_to_all | solution.py:306
  99.9 0.0 copy-done.9
  99.9 0.0 copy-done.5
  99.9 0.0 copy-done.8
  99.9 3.7 %tail.1 = f32[16,16,2048]{2,1,0:T(8,128)} custom-call(f32[2048,128]{1,0:T(8,128)S(1)} %bitcast.11, bf16[512,512]{1,0:T(8,128)(2,1)S(1)} %copy-done.5, bf16[1024,512]{1,0:T(8,128)(2,1)S(1)} %copy-done.9, bf16[1024,512]{1,0:T(8,128)(2,1)S(1)} %copy-done.8), custom_call_target="tpu_custom_call" | custom-call | flops 2000000000 | bytes 6000000 | tf_op jit(solution)/shard_map/tail/pallas_call | solution.py:307
Async XLA Ops:
  8.7 15.7 %copy-start.1 = (s32[512]{0:T(512)S(1)}, s32[512]{0:T(512)}, u32[]{:S(2)}) copy-start(s32[512]{0:T(512)} %param.13) | copy-start | bytes 6148
  8.7 15.8 %copy-start = (f32[2,512,512]{2,1,0:T(8,128)S(1)}, f32[2,512,512]{2,1,0:T(8,128)}, u32[]{:S(2)}) copy-start(f32[2,512,512]{2,1,0:T(8,128)} %p_ref.1) | copy-start | bytes 6291460
  8.7 46.6 %copy-start.10 = (f32[64]{0:T(128)S(1)}, f32[64]{0:T(128)}, u32[]{:S(2)}) copy-start(f32[64]{0:T(128)} %param.17) | copy-start | bytes 772
  8.7 46.7 %copy-start.6 = (f32[64,64]{1,0:T(8,128)S(1)}, f32[64,64]{1,0:T(8,128)}, u32[]{:S(2)}) copy-start(f32[64,64]{1,0:T(8,128)} %to_ref.1) | copy-start | bytes 49156
  8.7 46.7 %copy-start.7 = (f32[64,64]{1,0:T(8,128)S(1)}, f32[64,64]{1,0:T(8,128)}, u32[]{:S(2)}) copy-start(f32[64,64]{1,0:T(8,128)} %from_ref.1) | copy-start | bytes 49156
  8.7 46.6 %all-to-all-start = ((f32[256,8,128]{2,1,0:T(8,128)}), f32[256,8,128]{2,1,0:T(8,128)S(1)}, u32[]{:S(2)}, u32[]{:S(2)}) async-start(f32[256,8,128]{2,1,0:T(8,128)} %bitcast.14), calls=%async_computation | async-start | bytes 2097152 | tf_op jit(solution)/shard_map/all_to_all | solution.py:288
  25.2 1.0 copy-start.2
  26.2 1.0 copy-start.3
  27.2 0.8 copy-start.4
  55.4 44.5 %copy-start.9 = (bf16[1024,512]{1,0:T(8,128)(2,1)S(1)}, bf16[1024,512]{1,0:T(8,128)(2,1)}, u32[]{:S(2)}) copy-start(bf16[1024,512]{1,0:T(8,128)(2,1)} %constant.21.clone.high_hbm.high_ref) | copy-start | bytes 3145732
  62.5 37.3 %copy-start.5 = (bf16[512,512]{1,0:T(8,128)(2,1)S(1)}, bf16[512,512]{1,0:T(8,128)(2,1)}, u32[]{:S(2)}) copy-start(bf16[512,512]{1,0:T(8,128)(2,1)} %copy-done.4) | copy-start | bytes 1572868
  62.6 37.3 %copy-start.8 = (bf16[1024,512]{1,0:T(8,128)(2,1)S(1)}, bf16[1024,512]{1,0:T(8,128)(2,1)}, u32[]{:S(2)}) copy-start(bf16[1024,512]{1,0:T(8,128)(2,1)} %constant.22.clone.low_hbm.low_ref) | copy-start | bytes 3145732

commit v2 on v1

v2 whole, which is shorter than its diff:
```python
import jax
import jax.numpy as jnp
import numpy as np
from jax import lax
from jax.experimental import pallas as pl
from jax.experimental.pallas import tpu as pltpu
from jax.sharding import PartitionSpec as P

WAVES = 512
LON = 2048
QUARTER = LON // 4
RESIDUES = (0, 2, 1, 3)
BF16 = jnp.bfloat16
F32 = jnp.float32


def wave_rows():
    j = np.arange(QUARTER, dtype=np.int64)
    blocks = []
    for residue in RESIDUES:
        m = 4 * np.arange(WAVES // 4, dtype=np.int64) + residue
        angle = (m[:, None] * j[None, :] % LON) * (2.0 * np.pi / LON)
        blocks += [np.cos(angle), -np.sin(angle)]
    table = (np.concatenate(blocks, axis=0) * LON**-0.5).astype(np.float32)
    table = np.stack([table[:, : QUARTER // 2], table[:, QUARTER // 2 :]])
    high = table.astype(jnp.bfloat16)
    low = (table - high.astype(np.float32)).astype(jnp.bfloat16)
    return high, low


def split(value):
    high = value.astype(BF16)
    low = (value - high.astype(F32)).astype(BF16)
    return high, low


def mm(a, b):
    return lax.dot_general(a, b, (((1,), (0,)), ((), ())), preferred_element_type=F32)


def mm_nt(a, b):
    return lax.dot_general(a, b, (((1,), (1,)), ((), ())), preferred_element_type=F32)


def mm3(a, b):
    return mm(a[0], b[0]) + (mm(a[0], b[1]) + mm(a[1], b[0]))


def mm3_nt(a, b):
    return mm_nt(a[0], b[0]) + (mm_nt(a[0], b[1]) + mm_nt(a[1], b[0]))


def one_hot(slots_row):
    held = jnp.transpose(jnp.broadcast_to(slots_row.astype(F32), (128, WAVES)))
    lane = lax.broadcasted_iota(jnp.int32, (WAVES, 128), 1).astype(F32) * 4.0
    return jnp.concatenate(
        [(held == lane + float(r)).astype(F32).astype(BF16) for r in RESIDUES], axis=1
    )


def head_kernel(
    slots_hbm, grid_hbm, traj_hbm, high_hbm, low_hbm, out_hbm,
    slots_ref, grid_ref, traj_ref, high_ref, low_ref, parts, sent, sems,
):
    slots = pltpu.make_async_copy(slots_hbm, slots_ref, sems.at[40])
    slots.start()
    inputs, tables = [], []
    for half in range(2):
        for q in range(4):
            columns, at = pl.ds(QUARTER * q + QUARTER // 2 * half, QUARTER // 2), 4 * half + q
            for k, (src, dst) in enumerate(((grid_hbm, grid_ref), (traj_hbm, traj_ref))):
                inputs.append(pltpu.make_async_copy(src.at[:, columns], dst.at[at], sems.at[2 * at + k]))
                inputs[-1].start()
        for k, (src, dst) in enumerate(((high_hbm, high_ref), (low_hbm, low_ref))):
            tables.append(pltpu.make_async_copy(src.at[half], dst.at[half], sems.at[32 + 2 * half + k]))
            tables[-1].start()
    slots.wait()
    pick = one_hot(slots_ref[...])

    def product(half, a, b, n):
        count = b - a
        both = jnp.concatenate([high_ref[half, a:b, :], low_ref[half, a:b, :]], axis=0)
        wide = mm_nt(both, parts[half, n, 0])
        return wide[:count] + wide[count:] + mm_nt(high_ref[half, a:b, :], parts[half, n, 1])

    def fetch(half):
        for copy in inputs[8 * half : 8 * half + 8] + tables[2 * half : 2 * half + 2]:
            copy.wait()

    def combine(half):
        for lat in range(0, 16, 2):
            for h in range(2):
                quarters = []
                for q in range(4):
                    picked = [
                        jnp.concatenate([ref[4 * half + q, 16 * n + 8 * h : 16 * n + 8 * h + 8, :] for n in (lat, lat + 1)])
                        for ref in (grid_ref, traj_ref)
                    ]
                    quarters.append(picked[0] * (1.0 + picked[1]))
                q0, q1, q2, q3 = quarters
                even, swing = q0 + q2, q1 + q3
                rows = pl.ds(128 * h + 8 * lat, 16)
                for n, part in enumerate((even + swing, even - swing, q0 - q2, q1 - q3)):
                    parts[half, n, 0, rows, :], parts[half, n, 1, rows, :] = split(part)

    def products(half):
        return [product(half, a, b, n) for n, (a, b) in enumerate(((0, 256), (256, 512), (512, 1024), (512, 1024)))]

    fetch(0)
    combine(0)
    sums = products(0)
    fetch(1)
    combine(1)
    sums = [x + y for x, y in zip(sums, products(1))]
    zero, two, u1, u2 = sums
    cosine = [zero[:128], two[:128], u1[:128] + u2[128:256], u1[256:384] - u2[384:]]
    sine = [zero[128:], two[128:], u1[128:256] - u2[:128], u1[384:] + u2[256:384]]
    sides = [split(jnp.concatenate(wave, axis=0)) for wave in (cosine, sine)]
    wide = jnp.concatenate([sides[0][0], sides[1][0], sides[0][1], sides[1][1]], axis=1)
    stores = []
    for n in range(4):
        found = mm(pick[128 * n : 128 * (n + 1)], wide)
        found = found[:, :512] + found[:, 512:]
        for c in range(2):
            for k in range(2):
                sent[pl.ds(512 * n + 2 * k + c, 128, stride=4), :] = found[:, 256 * c + 128 * k : 256 * c + 128 * (k + 1)]
        rows = pl.ds(512 * n, 512)
        stores.append(pltpu.make_async_copy(sent.at[rows], out_hbm.at[rows], sems.at[36 + n]))
        stores[-1].start()
    for copy in stores:
        copy.wait()


def prepare_kernel(slots_ref, p_ref, to_ref, from_ref, high_ref, low_ref, pick_ref, couple_ref):
    for n, ref in enumerate((to_ref, from_ref)):
        high, low = split(ref[...])
        couple_ref[n] = jnp.concatenate([high, high, low], axis=1)
    source = lax.broadcasted_iota(jnp.int32, (128, 128), 0)
    target = lax.broadcasted_iota(jnp.int32, (128, 128), 1)
    order = (source == (target % 8) * 16 + target // 8).astype(F32).astype(BF16)
    for s in range(2):
        for ref, value in zip((high_ref, low_ref), split(p_ref[s])):
            for g in range(4):
                lanes = slice(128 * g, 128 * (g + 1))
                ref[s, :, lanes] = mm(value[:, lanes], order).astype(BF16)
    pick_ref[...] = one_hot(slots_ref[...])


def swap_groups(tiles, lane):
    tiles = list(tiles)
    for bit in (1, 2, 4):
        mask = (lane & bit) != 0
        for i in range(8):
            if i & bit:
                continue
            a, b = tiles[i], tiles[i | bit]
            moved = jnp.take_along_axis(jnp.where(mask, a, b), lane ^ bit, axis=1)
            tiles[i], tiles[i | bit] = jnp.where(mask, moved, a), jnp.where(mask, b, moved)
    return tiles


def mid_kernel(
    waves_ref, rates_ref, couple_ref, y_ref, ph_hbm, pl_hbm, state_hbm,
    spectral_hbm, z_ref,
    ph_ref, pl_ref, state_ref, spectral_ref, scale_ref, folds, north, south, sems,
):
    sources, targets = (ph_hbm, pl_hbm, state_hbm), (ph_ref, pl_ref, state_ref)
    copies = [pltpu.make_async_copy(a, b, sems.at[k]) for k, (a, b) in enumerate(zip(sources, targets))]
    for copy in copies:
        copy.start()
    lane = lax.broadcasted_iota(jnp.int32, (8, 128), 1)
    mirror = lane ^ 120
    flip = lambda tile: jnp.take_along_axis(tile, mirror, axis=1)

    def fold_step(step, carry):
        v, g = step // 4, step % 4
        ahead = swap_groups([y_ref[(8 * g + i) * 4 + v] for i in range(8)], lane)
        behind = swap_groups([y_ref[(63 - 8 * g - i) * 4 + v] for i in range(8)], lane)
        for j in range(8):
            a, b = ahead[j], flip(behind[j])
            rows = pl.ds(pl.multiple_of(64 * v + 8 * j, 8), 8)
            folds[0, g, rows, :] = a + b
            folds[1, g, rows, :] = a - b
        return carry

    lax.fori_loop(0, 16, fold_step, 0, unroll=4)
    k_row = lax.broadcasted_iota(jnp.int32, (1, WAVES), 1)
    even_k = k_row % 2 == 0
    rate = jnp.broadcast_to(rates_ref[:, 0:1], (64, WAVES))
    for s in range(2):
        degree = (k_row + waves_ref[s : s + 1, :]).astype(F32)
        helm = degree * (degree + 1.0) / (WAVES * (WAVES - 1.0))
        scale_ref[s] = 1.0 / (1.0 + helm * rate)
    for copy in copies:
        copy.wait()
    totals = []
    for s in range(2):
        fold = []
        for par in range(2):
            for c in range(2):
                halves = [
                    jnp.concatenate(
                        [folds[par, g, pl.ds(4 * s + 2 * h + c, 32, stride=8), :] for g in range(4)], axis=1
                    )
                    for h in range(2)
                ]
                fold += [halves[h][8 * v : 8 * v + 8] for v in range(4) for h in range(2)]
        both = mm3_nt(split(jnp.concatenate(fold, axis=0)), (ph_ref[s], pl_ref[s]))
        valid = (k_row < WAVES - waves_ref[s : s + 1, :]).astype(F32)
        mixed = jnp.where(even_k, both[:128], both[128:])
        total = (mixed + state_ref[pl.ds(128 * s, 128), :]) * valid
        totals += [total[:64], total[64:]]
    h, l = split(jnp.concatenate(totals, axis=1))
    modes = mm(couple_ref[0], jnp.concatenate([h, l, h], axis=0))
    scales = [scale_ref[s] for s in (0, 0, 1, 1)]
    h, l = split(modes * jnp.concatenate(scales, axis=1))
    spectral = mm(couple_ref[1], jnp.concatenate([h, l, h], axis=0))
    for n in range(4):
        spectral_ref[pl.ds(64 * n, 64), :] = spectral[:, WAVES * n : WAVES * (n + 1)]
    store = pltpu.make_async_copy(spectral_ref, spectral_hbm, sems.at[3])
    store.start()
    for s in range(2):
        own = spectral_ref[128 * s : 128 * (s + 1), :]
        pair = jnp.concatenate([jnp.where(even_k, own, 0.0), jnp.where(even_k, 0.0, own)], axis=0)
        both = mm3(split(pair), (ph_ref[s], pl_ref[s]))
        for to, side in ((north, both[:128] + both[128:]), (south, both[:128] - both[128:])):
            for c in range(2):
                for v in range(4):
                    for h in range(2):
                        row, start = 128 * s + 64 * h + 32 * c + 8 * v, 64 * c + 16 * v + 8 * h
                        for g in range(4):
                            to[g, row : row + 8, :] = side[start : start + 8, 128 * g : 128 * (g + 1)]
    for v in range(4):
        for g in range(4):
            for side in (north, south):
                tiles = [side[g, pl.ds(v * 8 + j, 8, stride=32), :] for j in range(8)]
                for i, tile in enumerate(swap_groups(tiles, lane)):
                    if side is north:
                        z_ref[(8 * g + i) * 4 + v] = tile
                    else:
                        z_ref[(63 - 8 * g - i) * 4 + v] = flip(tile)
    store.wait()


def tail_kernel(z_ref, pick_ref, high_ref, low_ref, out_hbm, block, sems):
    pick = pick_ref[...]
    natural = []
    for c in range(2):
        sides = [z_ref[pl.ds(2 * k + c, WAVES, stride=4), :] for k in range(2)]
        h, l = split(jnp.transpose(jnp.concatenate(sides, axis=1)))
        natural.append(split(mm(h, pick) + mm(l, pick)))
    part = lambda c, kind: tuple(natural[c][n][:, 128 * kind : 128 * (kind + 1)] for n in range(2))
    minus = lambda pair: (-pair[0], -pair[1])
    join = lambda *parts: tuple(jnp.concatenate([p[n] for p in parts], axis=1) for n in range(2))
    whole = lambda ref, a, b: jnp.concatenate([ref[0, a:b, :], ref[1, a:b, :]], axis=1)
    table = lambda a, b: (whole(high_ref, a, b), whole(low_ref, a, b))
    zero = mm3(join(part(0, 0), part(1, 0)), table(0, 256))
    two = mm3(join(part(0, 1), part(1, 1)), table(256, 512))
    odd = table(512, 1024)
    stores = []

    def put(q, value):
        for h in range(2):
            for lat in range(16):
                row = 128 * h + 8 * lat
                block[lat, 8 * h : 8 * h + 8, QUARTER * q : QUARTER * (q + 1)] = value[row : row + 8]
        columns = pl.ds(QUARTER * q, QUARTER)
        stores.append(pltpu.make_async_copy(block.at[:, :, columns], out_hbm.at[:, :, columns], sems.at[q]))
        stores[-1].start()

    plus, less = zero + two, zero - two
    first = mm3(join(part(0, 2), part(1, 2), part(0, 3), part(1, 3)), odd)
    put(0, plus + first)
    put(2, plus - first)
    turned = mm3(join(minus(part(1, 2)), part(0, 2), part(1, 3), minus(part(0, 3))), odd)
    put(1, less + turned)
    put(3, less - turned)
    for copy in stores:
        copy.wait()


VMEM = pl.BlockSpec(memory_space=pltpu.VMEM)
HBM = pl.BlockSpec(memory_space=pltpu.HBM)
DMA = pltpu.SemaphoreType.DMA


def call(kernel, name, outs, in_specs, out_specs, scratch=(), flops=0, moved=0, room=32):
    return pl.pallas_call(
        kernel,
        name=name,
        out_shape=outs,
        in_specs=in_specs,
        out_specs=out_specs,
        scratch_shapes=list(scratch),
        compiler_params=pltpu.CompilerParams(vmem_limit_bytes=room * 2**20),
        cost_estimate=pl.CostEstimate(flops=flops, bytes_accessed=moved, transcendentals=0),
    )


def shards(grid_adjoint, trajectory, legendre_north, slot_wavenumber, spectral_state, to_modes, from_modes, rates):
    shape = jax.ShapeDtypeStruct
    high, low = wave_rows()
    high, low = jnp.asarray(high), jnp.asarray(low)
    slots_row = slot_wavenumber.reshape(1, WAVES)
    device = lax.axis_index("band") * lax.axis_size("lev") + lax.axis_index("lev")
    own_waves = lax.dynamic_slice_in_dim(slot_wavenumber, 2 * device, 2)

    square = (256, LON)
    sent = call(
        head_kernel, "head", shape((2048, 128), F32), [HBM] * 5, HBM,
        [pltpu.VMEM((1, WAVES), jnp.int32)] + [pltpu.VMEM((8, 256, QUARTER // 2), F32)] * 2 + [pltpu.VMEM((2, 1024, QUARTER // 2), BF16)] * 2
        + [pltpu.VMEM((2, 4, 2, 256, QUARTER // 2), BF16), pltpu.VMEM((2048, 128), F32), DMA((41,))],
        flops=2 * 10**9, moved=7 * 10**6, room=60,
    )(slots_row, grid_adjoint.reshape(square), trajectory.reshape(square), high, low)
    arrived = lax.all_to_all(sent.reshape(256, 8, 128), ("band", "lev"), 0, 0, tiled=True)

    ph, plo, pick, couple = call(
        prepare_kernel, "prepare",
        [shape((2, 512, 512), BF16)] * 2 + [shape((512, 512), BF16), shape((2, 64, 192), BF16)],
        [VMEM] * 4, [VMEM] * 4, flops=10**8, moved=8 * 10**6,
    )(slots_row, legendre_north, to_modes, from_modes)
    state = jnp.transpose(spectral_state, (0, 2, 3, 1)).reshape(256, WAVES)
    columns = jnp.broadcast_to(rates[:, None], (64, 128))
    far = [pltpu.with_memory_space_constraint(v, pltpu.HBM) for v in (ph, plo, state)]

    legendre, rows = pltpu.VMEM((2, 512, 512), BF16), pltpu.VMEM((256, WAVES), F32)
    spectral, back = call(
        mid_kernel, "mid", [shape((256, WAVES), F32), shape((256, 8, 128), F32)],
        [VMEM] * 4 + [HBM] * 3, [HBM, VMEM],
        [legendre, legendre, rows, rows, pltpu.VMEM((2, 64, WAVES), F32), pltpu.VMEM((2, 4, 256, 128), F32)]
        + [pltpu.VMEM((4, 256, 128), F32)] * 2 + [DMA((4,))],
        flops=3 * 10**9, moved=8 * 10**6, room=32,
    )(jnp.broadcast_to(own_waves[:, None], (2, WAVES)), columns, couple, arrived, *far)
    returned = lax.all_to_all(back, ("band", "lev"), 0, 0, tiled=True)
    grid = call(
        tail_kernel, "tail", shape((16, 16, LON), F32), [VMEM] * 4, HBM,
        [pltpu.VMEM((16, 16, LON), F32), DMA((4,))],
        flops=2 * 10**9, moved=6 * 10**6,
    )(returned.reshape(2048, 128), pick, high, low)
    spectral_out = jnp.transpose(spectral.reshape(2, 2, 64, WAVES), (0, 3, 1, 2))
    return spectral_out, grid


def solution(mesh):
    spread = P(("band", "lev"), None, None)
    return jax.shard_map(
        shards,
        mesh=mesh,
        in_specs=(
            P("band", "lev", None), P("band", "lev", None), spread, P(),
            P(("band", "lev"), None, None, None), P(), P(), P(),
        ),
        out_specs=(P(("band", "lev"), None, None, None), P("band", "lev", None)),
        check_vma=False,
    )
```

time: 104 us -> 99.7 us (0.959)
  Pallas kernels: 19.6 us -> 15.5 us
    pallas_call x1, Pallas kernels: 7.1 us -> 5.27 us  [shards(): call(mid_kernel, 'mid', [shape((256, WAVES), F32), shape((256, 8, 128), F...]
    pallas_call x1, Pallas kernels: 8.04 us -> 6.35 us  [shards(): call(head_kernel, 'head', shape((2048, 128), F32), [HBM] * 5, HBM, [pltpu...]
where the time goes in v2:
time: 99.7 us; the launch traced here: 99.6 us
  blocking collectives  37.3 us (37%)
  waiting for transfers between devices  27.3 us (27%)
  starting transfers between devices  15.7 us (16%)
  Pallas kernels  15.5 us (16%)
  local copies, waits for them, and re-layouts  3.03 us (3%)
    all_to_all x1, blocking collectives, shards(): returned = lax.all_to_all(back, ('band', 'lev'), 0, 0, tiled=True)  37.3 us
    all_to_all x1, waiting for transfers between devices, shards(): lax.all_to_all(sent.reshape(256, 8, 128), ('band', 'lev'), 0, 0, tiled=True)  27.3 us
    all_to_all x1, starting transfers between devices, shards(): lax.all_to_all(sent.reshape(256, 8, 128), ('band', 'lev'), 0, 0, tiled=True)  15.7 us
    pallas_call x1, Pallas kernels, shards(): call(head_kernel, 'head', shape((2048, 128), F32), [HBM] * 5, HBM, [pltpu...  6.35 us
    pallas_call x1, Pallas kernels, shards(): call(mid_kernel, 'mid', [shape((256, WAVES), F32), shape((256, 8, 128), F...  5.27 us
    pallas_call x1, Pallas kernels, shards(): call(tail_kernel, 'tail', shape((16, 16, LON), F32), [VMEM] * 4, HBM, [pl...  3.15 us
    unnamed x22, local copies, waits for them, and re-layouts  2.81 us
  transfers between devices with their start and end apart: 1, of which 1 were waited for; matrix products, arithmetic and copies ran while one was open for 0% of the time, Pallas kernels for 1%

profile of v2, /device:TPU:1, one launch (start us, length us, event | category | flops | bytes accessed | tf_op | source)
XLA Modules:
  0.0 99.6 jit_solution(10226883341910992564)
XLA Ops:
  0.6 0.0 copy-start.1
  0.6 0.0 copy-start.2
  0.7 6.3 %head.1 = f32[2048,128]{1,0:T(8,128)} custom-call(s32[1,512]{1,0:T(1,128)} %bitcast.12, f32[256,2048]{1,0:T(8,128)} %bitcast.15, f32[256,2048]{1,0:T(8,128)} %bitcast.16, bf16[2,1024,256]{2,1,0:T(8,128)(2,1)} %constant.21.clone.high_hbm.high_ref, bf16[2,1024,256]{2,1,0:T(8,128)(2,1)} %constant.22.clone.low_hbm.low_ref), custom_call_target="tpu_custom_call" | custom-call | flops 2000000000 | bytes 7000000 | tf_op jit(solution)/shard_map/head/pallas_call | solution.py:309
  7.0 0.0 copy-start.3
  7.0 0.0 copy-start
  7.0 0.0 copy-start.10
  7.0 15.7 %all-to-all-start = ((f32[256,8,128]{2,1,0:T(8,128)}), f32[256,8,128]{2,1,0:T(8,128)S(1)}, u32[]{:S(2)}, u32[]{:S(2)}) async-start(f32[256,8,128]{2,1,0:T(8,128)} %bitcast.14), calls=%async_computation | async-start | bytes 2097152 | tf_op jit(solution)/shard_map/all_to_all | solution.py:315
  22.7 0.0 copy-done.3
  22.7 0.1 dynamic_slice.3
  22.8 0.0 copy-done.1
  22.8 0.0 copy-done.2
  22.8 0.0 copy-done
  22.8 0.7 prepare.1
  23.5 0.0 copy-start.4
  23.5 1.0 copy-done.4
  24.5 0.0 copy-start.5
  24.5 1.0 copy-done.5
  25.5 0.0 copy-start.6
  25.5 0.8 copy-done.6
  26.3 27.3 %all-to-all-done.y_ref = f32[256,8,128]{2,1,0:T(8,128)S(1)} async-done(((f32[256,8,128]{2,1,0:T(8,128)}), f32[256,8,128]{2,1,0:T(8,128)S(1)}, u32[]{:S(2)}, u32[]{:S(2)}) %all-to-all-start) | async-done | bytes 1048608 | tf_op jit(solution)/shard_map/all_to_all | solution.py:315
  53.7 0.1 broadcast_in_dim.4.waves_ref
  53.7 0.0 copy-done.10
  53.7 0.1 broadcast_in_dim.5.rates_ref
  53.8 0.0 copy-start.9
  53.8 5.3 %mid.1 = (f32[256,512]{1,0:T(8,128)}, f32[256,8,128]{2,1,0:T(8,128)S(1)}) custom-call(s32[2,512]{1,0:T(2,128)S(1)} %broadcast_in_dim.4.waves_ref, f32[64,128]{1,0:T(8,128)S(1)} %broadcast_in_dim.5.rates_ref, bf16[2,64,192]{2,1,0:T(8,128)(2,1)S(1)} %get-tuple-element.8.couple_ref, f32[256,8,128]{2,1,0:T(8,128)S(1)} %all-to-all-done.y_ref, ...), custom_call_target="tpu_custom_call" | custom-call | flops 3000000000 | bytes 8000000 | tf_op jit(solution)/shard_map/mid/pallas_call | solution.py:327
  59.1 0.0 copy-start.7
  59.1 0.0 copy-start.8
  59.1 37.3 %all_to_all.10 = f32[256,8,128]{2,1,0:T(8,128)S(1)} all-to-all(f32[256,8,128]{2,1,0:T(8,128)S(1)} %get-tuple-element.12), channel_id=1, replica_groups=mesh['band'=64,'lev'=4] {'band','lev'}, dimensions={0} | all-to-all | bytes 2097152 | tf_op jit(solution)/shard_map/all_to_all | solution.py:334
  96.4 0.0 copy-done.9
  96.4 0.0 copy-done.7
  96.4 0.0 copy-done.8
  96.4 3.1 %tail.1 = f32[16,16,2048]{2,1,0:T(8,128)} custom-call(f32[2048,128]{1,0:T(8,128)S(1)} %bitcast.11, bf16[512,512]{1,0:T(8,128)(2,1)S(1)} %copy-done.7, bf16[2,1024,256]{2,1,0:T(8,128)(2,1)S(1)} %copy-done.9, bf16[2,1024,256]{2,1,0:T(8,128)(2,1)S(1)} %copy-done.8), custom_call_target="tpu_custom_call" | custom-call | flops 2000000000 | bytes 6000000 | tf_op jit(solution)/shard_map/tail/pallas_call | solution.py:335
Async XLA Ops:
  0.6 22.2 %copy-start.1 = (f32[64,64]{1,0:T(8,128)S(1)}, f32[64,64]{1,0:T(8,128)}, u32[]{:S(2)}) copy-start(f32[64,64]{1,0:T(8,128)} %to_ref.1) | copy-start | bytes 49156
  0.6 22.2 %copy-start.2 = (f32[64,64]{1,0:T(8,128)S(1)}, f32[64,64]{1,0:T(8,128)}, u32[]{:S(2)}) copy-start(f32[64,64]{1,0:T(8,128)} %from_ref.1) | copy-start | bytes 49156
  7.0 15.7 %copy-start.3 = (s32[512]{0:T(512)S(1)}, s32[512]{0:T(512)}, u32[]{:S(2)}) copy-start(s32[512]{0:T(512)} %param.13) | copy-start | bytes 6148
  7.0 15.8 %copy-start = (f32[2,512,512]{2,1,0:T(8,128)S(1)}, f32[2,512,512]{2,1,0:T(8,128)}, u32[]{:S(2)}) copy-start(f32[2,512,512]{2,1,0:T(8,128)} %p_ref.1) | copy-start | bytes 6291460
  7.0 46.7 %copy-start.10 = (f32[64]{0:T(128)S(1)}, f32[64]{0:T(128)}, u32[]{:S(2)}) copy-start(f32[64]{0:T(128)} %param.17) | copy-start | bytes 772
  7.0 46.6 %all-to-all-start = ((f32[256,8,128]{2,1,0:T(8,128)}), f32[256,8,128]{2,1,0:T(8,128)S(1)}, u32[]{:S(2)}, u32[]{:S(2)}) async-start(f32[256,8,128]{2,1,0:T(8,128)} %bitcast.14), calls=%async_computation | async-start | bytes 2097152 | tf_op jit(solution)/shard_map/all_to_all | solution.py:315
  23.5 1.0 copy-start.4
  24.5 1.0 %copy-start.5 = (bf16[2,512,512]{2,1,0:T(8,128)(2,1)}, bf16[2,512,512]{2,1,0:T(8,128)(2,1)S(1)}, u32[]{:S(2)}) copy-start(bf16[2,512,512]{2,1,0:T(8,128)(2,1)S(1)} %get-tuple-element.10.pl_hbm) | copy-start | bytes 3145732
  25.5 0.8 copy-start.6
  53.8 42.6 %copy-start.9 = (bf16[2,1024,256]{2,1,0:T(8,128)(2,1)S(1)}, bf16[2,1024,256]{2,1,0:T(8,128)(2,1)}, u32[]{:S(2)}) copy-start(bf16[2,1024,256]{2,1,0:T(8,128)(2,1)} %constant.21.clone.high_hbm.high_ref) | copy-start | bytes 3145732
  59.1 37.3 %copy-start.7 = (bf16[512,512]{1,0:T(8,128)(2,1)S(1)}, bf16[512,512]{1,0:T(8,128)(2,1)}, u32[]{:S(2)}) copy-start(bf16[512,512]{1,0:T(8,128)(2,1)} %copy-done.6) | copy-start | bytes 1572868
  59.1 37.3 %copy-start.8 = (bf16[2,1024,256]{2,1,0:T(8,128)(2,1)S(1)}, bf16[2,1024,256]{2,1,0:T(8,128)(2,1)}, u32[]{:S(2)}) copy-start(bf16[2,1024,256]{2,1,0:T(8,128)(2,1)} %constant.22.clone.low_hbm.low_ref) | copy-start | bytes 3145732

commit v3 on v2

--- a/solution.py
+++ b/solution.py
@@ -10,6 +10,7 @@
 LON = 2048
 QUARTER = LON // 4
 RESIDUES = (0, 2, 1, 3)
+PITCH = 40
 BF16 = jnp.bfloat16
 F32 = jnp.float32
 
@@ -84,7 +85,7 @@
         return wide[:count] + wide[count:] + mm_nt(high_ref[half, a:b, :], parts[half, n, 1])
 
     def fetch(half):
-        for copy in inputs[8 * half : 8 * half + 8] + tables[2 * half : 2 * half + 2]:
+        for copy in inputs[8 * half : 8 * half + 8]:
             copy.wait()
 
     def combine(half):
@@ -104,6 +105,8 @@
                     parts[half, n, 0, rows, :], parts[half, n, 1, rows, :] = split(part)
 
     def products(half):
+        for copy in tables[2 * half : 2 * half + 2]:
+            copy.wait()
         return [product(half, a, b, n) for n, (a, b) in enumerate(((0, 256), (256, 512), (512, 1024), (512, 1024)))]
 
     fetch(0)
@@ -227,13 +230,13 @@
             for c in range(2):
                 for v in range(4):
                     for h in range(2):
-                        row, start = 128 * s + 64 * h + 32 * c + 8 * v, 64 * c + 16 * v + 8 * h
+                        row, start = PITCH * (4 * s + 2 * h + c) + 8 * v, 64 * c + 16 * v + 8 * h
                         for g in range(4):
                             to[g, row : row + 8, :] = side[start : start + 8, 128 * g : 128 * (g + 1)]
     for v in range(4):
         for g in range(4):
             for side in (north, south):
-                tiles = [side[g, pl.ds(v * 8 + j, 8, stride=32), :] for j in range(8)]
+                tiles = [side[g, pl.ds(v * 8 + j, 8, stride=PITCH), :] for j in range(8)]
                 for i, tile in enumerate(swap_groups(tiles, lane)):
                     if side is north:
                         z_ref[(8 * g + i) * 4 + v] = tile
@@ -328,7 +331,7 @@
         mid_kernel, "mid", [shape((256, WAVES), F32), shape((256, 8, 128), F32)],
         [VMEM] * 4 + [HBM] * 3, [HBM, VMEM],
         [legendre, legendre, rows, rows, pltpu.VMEM((2, 64, WAVES), F32), pltpu.VMEM((2, 4, 256, 128), F32)]
-        + [pltpu.VMEM((4, 256, 128), F32)] * 2 + [DMA((4,))],
+        + [pltpu.VMEM((4, 8 * PITCH, 128), F32)] * 2 + [DMA((4,))],
         flops=3 * 10**9, moved=8 * 10**6, room=32,
     )(jnp.broadcast_to(own_waves[:, None], (2, WAVES)), columns, couple, arrived, *far)
     returned = lax.all_to_all(back, ("band", "lev"), 0, 0, tiled=True)

time: 99.7 us -> 99.3 us (level)
  no operation moved by 1% of the time
where the time goes in v3:
time: 99.3 us; the launch traced here: 99.2 us
  blocking collectives  37.3 us (38%)
  waiting for transfers between devices  27.3 us (27%)
  starting transfers between devices  15.7 us (16%)
  Pallas kernels  15.1 us (15%)
  local copies, waits for them, and re-layouts  3.03 us (3%)
    all_to_all x1, blocking collectives, shards(): returned = lax.all_to_all(back, ('band', 'lev'), 0, 0, tiled=True)  37.3 us
    all_to_all x1, waiting for transfers between devices, shards(): lax.all_to_all(sent.reshape(256, 8, 128), ('band', 'lev'), 0, 0, tiled=True)  27.3 us
    all_to_all x1, starting transfers between devices, shards(): lax.all_to_all(sent.reshape(256, 8, 128), ('band', 'lev'), 0, 0, tiled=True)  15.7 us
    pallas_call x1, Pallas kernels, shards(): call(head_kernel, 'head', shape((2048, 128), F32), [HBM] * 5, HBM, [pltpu...  6.37 us
    pallas_call x1, Pallas kernels, shards(): call(mid_kernel, 'mid', [shape((256, WAVES), F32), shape((256, 8, 128), F...  4.84 us
    pallas_call x1, Pallas kernels, shards(): call(tail_kernel, 'tail', shape((16, 16, LON), F32), [VMEM] * 4, HBM, [pl...  3.14 us
    unnamed x22, local copies, waits for them, and re-layouts  2.81 us
  transfers between devices with their start and end apart: 1, of which 1 were waited for; matrix products, arithmetic and copies ran while one was open for 0% of the time, Pallas kernels for 1%

profile of v3, /device:TPU:1, one launch (start us, length us, event | category | flops | bytes accessed | tf_op | source)
XLA Modules:
  0.0 99.2 jit_solution(5029011161263751400)
XLA Ops:
  0.6 0.0 copy-start.1
  0.6 0.0 copy-start.2
  0.7 6.4 %head.1 = f32[2048,128]{1,0:T(8,128)} custom-call(s32[1,512]{1,0:T(1,128)} %bitcast.12, f32[256,2048]{1,0:T(8,128)} %bitcast.15, f32[256,2048]{1,0:T(8,128)} %bitcast.16, bf16[2,1024,256]{2,1,0:T(8,128)(2,1)} %constant.21.clone.high_hbm.high_ref, bf16[2,1024,256]{2,1,0:T(8,128)(2,1)} %constant.22.clone.low_hbm.low_ref), custom_call_target="tpu_custom_call" | custom-call | flops 2000000000 | bytes 7000000 | tf_op jit(solution)/shard_map/head/pallas_call | solution.py:312
  7.0 0.0 copy-start.3
  7.0 0.0 copy-start
  7.0 0.0 copy-start.10
  7.1 15.7 %all-to-all-start = ((f32[256,8,128]{2,1,0:T(8,128)}), f32[256,8,128]{2,1,0:T(8,128)S(1)}, u32[]{:S(2)}, u32[]{:S(2)}) async-start(f32[256,8,128]{2,1,0:T(8,128)} %bitcast.14), calls=%async_computation | async-start | bytes 2097152 | tf_op jit(solution)/shard_map/all_to_all | solution.py:318
  22.7 0.0 copy-done.3
  22.7 0.1 dynamic_slice.3
  22.8 0.0 copy-done.1
  22.8 0.0 copy-done.2
  22.8 0.0 copy-done
  22.8 0.7 prepare.1
  23.5 0.0 copy-start.4
  23.6 1.0 copy-done.4
  24.5 0.0 copy-start.5
  24.5 1.0 %copy-done.5 = bf16[2,512,512]{2,1,0:T(8,128)(2,1)} copy-done((bf16[2,512,512]{2,1,0:T(8,128)(2,1)}, bf16[2,512,512]{2,1,0:T(8,128)(2,1)S(1)}, u32[]{:S(2)}) %copy-start.5) | copy-done | bytes 1048600
  25.5 0.0 copy-start.6
  25.5 0.8 copy-done.6
  26.3 27.3 %all-to-all-done.y_ref = f32[256,8,128]{2,1,0:T(8,128)S(1)} async-done(((f32[256,8,128]{2,1,0:T(8,128)}), f32[256,8,128]{2,1,0:T(8,128)S(1)}, u32[]{:S(2)}, u32[]{:S(2)}) %all-to-all-start) | async-done | bytes 1048608 | tf_op jit(solution)/shard_map/all_to_all | solution.py:318
  53.7 0.1 broadcast_in_dim.4.waves_ref
  53.7 0.0 copy-done.10
  53.7 0.1 broadcast_in_dim.5.rates_ref
  53.8 0.0 copy-start.9
  53.8 4.8 %mid.1 = (f32[256,512]{1,0:T(8,128)}, f32[256,8,128]{2,1,0:T(8,128)S(1)}) custom-call(s32[2,512]{1,0:T(2,128)S(1)} %broadcast_in_dim.4.waves_ref, f32[64,128]{1,0:T(8,128)S(1)} %broadcast_in_dim.5.rates_ref, bf16[2,64,192]{2,1,0:T(8,128)(2,1)S(1)} %get-tuple-element.8.couple_ref, f32[256,8,128]{2,1,0:T(8,128)S(1)} %all-to-all-done.y_ref, ...), custom_call_target="tpu_custom_call" | custom-call | flops 3000000000 | bytes 8000000 | tf_op jit(solution)/shard_map/mid/pallas_call | solution.py:330
  58.7 0.0 copy-start.7
  58.7 0.0 copy-start.8
  58.7 37.3 %all_to_all.10 = f32[256,8,128]{2,1,0:T(8,128)S(1)} all-to-all(f32[256,8,128]{2,1,0:T(8,128)S(1)} %get-tuple-element.12), channel_id=1, replica_groups=mesh['band'=64,'lev'=4] {'band','lev'}, dimensions={0} | all-to-all | bytes 2097152 | tf_op jit(solution)/shard_map/all_to_all | solution.py:337
  96.0 0.0 copy-done.9
  96.0 0.0 copy-done.7
  96.0 0.0 copy-done.8
  96.0 3.1 %tail.1 = f32[16,16,2048]{2,1,0:T(8,128)} custom-call(f32[2048,128]{1,0:T(8,128)S(1)} %bitcast.11, bf16[512,512]{1,0:T(8,128)(2,1)S(1)} %copy-done.7, bf16[2,1024,256]{2,1,0:T(8,128)(2,1)S(1)} %copy-done.9, bf16[2,1024,256]{2,1,0:T(8,128)(2,1)S(1)} %copy-done.8), custom_call_target="tpu_custom_call" | custom-call | flops 2000000000 | bytes 6000000 | tf_op jit(solution)/shard_map/tail/pallas_call | solution.py:338
Async XLA Ops:
  0.6 22.2 %copy-start.1 = (f32[64,64]{1,0:T(8,128)S(1)}, f32[64,64]{1,0:T(8,128)}, u32[]{:S(2)}) copy-start(f32[64,64]{1,0:T(8,128)} %to_ref.1) | copy-start | bytes 49156
  0.6 22.2 %copy-start.2 = (f32[64,64]{1,0:T(8,128)S(1)}, f32[64,64]{1,0:T(8,128)}, u32[]{:S(2)}) copy-start(f32[64,64]{1,0:T(8,128)} %from_ref.1) | copy-start | bytes 49156
  7.0 15.7 %copy-start.3 = (s32[512]{0:T(512)S(1)}, s32[512]{0:T(512)}, u32[]{:S(2)}) copy-start(s32[512]{0:T(512)} %param.13) | copy-start | bytes 6148
  7.0 15.8 %copy-start = (f32[2,512,512]{2,1,0:T(8,128)S(1)}, f32[2,512,512]{2,1,0:T(8,128)}, u32[]{:S(2)}) copy-start(f32[2,512,512]{2,1,0:T(8,128)} %p_ref.1) | copy-start | bytes 6291460
  7.0 46.7 %copy-start.10 = (f32[64]{0:T(128)S(1)}, f32[64]{0:T(128)}, u32[]{:S(2)}) copy-start(f32[64]{0:T(128)} %param.17) | copy-start | bytes 772
  7.1 46.6 %all-to-all-start = ((f32[256,8,128]{2,1,0:T(8,128)}), f32[256,8,128]{2,1,0:T(8,128)S(1)}, u32[]{:S(2)}, u32[]{:S(2)}) async-start(f32[256,8,128]{2,1,0:T(8,128)} %bitcast.14), calls=%async_computation | async-start | bytes 2097152 | tf_op jit(solution)/shard_map/all_to_all | solution.py:318
  23.5 1.0 copy-start.4
  24.5 1.0 %copy-start.5 = (bf16[2,512,512]{2,1,0:T(8,128)(2,1)}, bf16[2,512,512]{2,1,0:T(8,128)(2,1)S(1)}, u32[]{:S(2)}) copy-start(bf16[2,512,512]{2,1,0:T(8,128)(2,1)S(1)} %get-tuple-element.10.pl_hbm) | copy-start | bytes 3145732
  25.5 0.8 copy-start.6
  53.8 42.2 %copy-start.9 = (bf16[2,1024,256]{2,1,0:T(8,128)(2,1)S(1)}, bf16[2,1024,256]{2,1,0:T(8,128)(2,1)}, u32[]{:S(2)}) copy-start(bf16[2,1024,256]{2,1,0:T(8,128)(2,1)} %constant.21.clone.high_hbm.high_ref) | copy-start | bytes 3145732
  58.7 37.3 %copy-start.7 = (bf16[512,512]{1,0:T(8,128)(2,1)S(1)}, bf16[512,512]{1,0:T(8,128)(2,1)}, u32[]{:S(2)}) copy-start(bf16[512,512]{1,0:T(8,128)(2,1)} %copy-done.6) | copy-start | bytes 1572868
  58.7 37.3 %copy-start.8 = (bf16[2,1024,256]{2,1,0:T(8,128)(2,1)S(1)}, bf16[2,1024,256]{2,1,0:T(8,128)(2,1)}, u32[]{:S(2)}) copy-start(bf16[2,1024,256]{2,1,0:T(8,128)(2,1)} %constant.22.clone.low_hbm.low_ref) | copy-start | bytes 3145732

commit v4 on v3

--- a/solution.py
+++ b/solution.py
@@ -57,6 +57,10 @@
     return jnp.concatenate(
         [(held == lane + float(r)).astype(F32).astype(BF16) for r in RESIDUES], axis=1
     )
+
+
+def south_mask():
+    return jnp.where(lax.axis_index("band") >= lax.axis_size("band") // 2, 15, 0)
 
 
 def head_kernel(
@@ -88,13 +92,16 @@
         for copy in inputs[8 * half : 8 * half + 8]:
             copy.wait()
 
+    reverse = south_mask()
+    level_rows = lambda lat, h: pl.ds(pl.multiple_of(16 * (lat ^ reverse) + 8 * h, 8), 8)
+
     def combine(half):
         for lat in range(0, 16, 2):
             for h in range(2):
                 quarters = []
                 for q in range(4):
                     picked = [
-                        jnp.concatenate([ref[4 * half + q, 16 * n + 8 * h : 16 * n + 8 * h + 8, :] for n in (lat, lat + 1)])
+                        jnp.concatenate([ref[4 * half + q, level_rows(n, h), :] for n in (lat, lat + 1)])
                         for ref in (grid_ref, traj_ref)
                     ]
                     quarters.append(picked[0] * (1.0 + picked[1]))
@@ -167,20 +174,21 @@
     spectral_hbm, z_ref,
     ph_ref, pl_ref, state_ref, spectral_ref, scale_ref, folds, north, south, sems,
 ):
-    sources, targets = (ph_hbm, pl_hbm, state_hbm), (ph_ref, pl_ref, state_ref)
-    copies = [pltpu.make_async_copy(a, b, sems.at[k]) for k, (a, b) in enumerate(zip(sources, targets))]
-    for copy in copies:
-        copy.start()
+    copies = []
+    for s in range(2):
+        rows = pl.ds(128 * s, 128)
+        pairs = ((ph_hbm.at[s], ph_ref.at[s]), (pl_hbm.at[s], pl_ref.at[s]), (state_hbm.at[rows], state_ref.at[rows]))
+        copies.append([pltpu.make_async_copy(a, b, sems.at[3 * s + k]) for k, (a, b) in enumerate(pairs)])
+        for copy in copies[s]:
+            copy.start()
     lane = lax.broadcasted_iota(jnp.int32, (8, 128), 1)
-    mirror = lane ^ 120
-    flip = lambda tile: jnp.take_along_axis(tile, mirror, axis=1)
 
     def fold_step(step, carry):
         v, g = step // 4, step % 4
         ahead = swap_groups([y_ref[(8 * g + i) * 4 + v] for i in range(8)], lane)
         behind = swap_groups([y_ref[(63 - 8 * g - i) * 4 + v] for i in range(8)], lane)
         for j in range(8):
-            a, b = ahead[j], flip(behind[j])
+            a, b = ahead[j], behind[j]
             rows = pl.ds(pl.multiple_of(64 * v + 8 * j, 8), 8)
             folds[0, g, rows, :] = a + b
             folds[1, g, rows, :] = a - b
@@ -194,10 +202,10 @@
         degree = (k_row + waves_ref[s : s + 1, :]).astype(F32)
         helm = degree * (degree + 1.0) / (WAVES * (WAVES - 1.0))
         scale_ref[s] = 1.0 / (1.0 + helm * rate)
-    for copy in copies:
-        copy.wait()
     totals = []
     for s in range(2):
+        for copy in copies[s]:
+            copy.wait()
         fold = []
         for par in range(2):
             for c in range(2):
@@ -220,7 +228,7 @@
     spectral = mm(couple_ref[1], jnp.concatenate([h, l, h], axis=0))
     for n in range(4):
         spectral_ref[pl.ds(64 * n, 64), :] = spectral[:, WAVES * n : WAVES * (n + 1)]
-    store = pltpu.make_async_copy(spectral_ref, spectral_hbm, sems.at[3])
+    store = pltpu.make_async_copy(spectral_ref, spectral_hbm, sems.at[6])
     store.start()
     for s in range(2):
         own = spectral_ref[128 * s : 128 * (s + 1), :]
@@ -241,7 +249,7 @@
                     if side is north:
                         z_ref[(8 * g + i) * 4 + v] = tile
                     else:
-                        z_ref[(63 - 8 * g - i) * 4 + v] = flip(tile)
+                        z_ref[(63 - 8 * g - i) * 4 + v] = tile
     store.wait()
 
 
@@ -261,12 +269,13 @@
     two = mm3(join(part(0, 1), part(1, 1)), table(256, 512))
     odd = table(512, 1024)
     stores = []
+    reverse = south_mask()
 
     def put(q, value):
         for h in range(2):
             for lat in range(16):
                 row = 128 * h + 8 * lat
-                block[lat, 8 * h : 8 * h + 8, QUARTER * q : QUARTER * (q + 1)] = value[row : row + 8]
+                block[lat ^ reverse, 8 * h : 8 * h + 8, QUARTER * q : QUARTER * (q + 1)] = value[row : row + 8]
         columns = pl.ds(QUARTER * q, QUARTER)
         stores.append(pltpu.make_async_copy(block.at[:, :, columns], out_hbm.at[:, :, columns], sems.at[q]))
         stores[-1].start()
@@ -331,7 +340,7 @@
         mid_kernel, "mid", [shape((256, WAVES), F32), shape((256, 8, 128), F32)],
         [VMEM] * 4 + [HBM] * 3, [HBM, VMEM],
         [legendre, legendre, rows, rows, pltpu.VMEM((2, 64, WAVES), F32), pltpu.VMEM((2, 4, 256, 128), F32)]
-        + [pltpu.VMEM((4, 8 * PITCH, 128), F32)] * 2 + [DMA((4,))],
+        + [pltpu.VMEM((4, 8 * PITCH, 128), F32)] * 2 + [DMA((7,))],
         flops=3 * 10**9, moved=8 * 10**6, room=32,
     )(jnp.broadcast_to(own_waves[:, None], (2, WAVES)), columns, couple, arrived, *far)
     returned = lax.all_to_all(back, ("band", "lev"), 0, 0, tiled=True)

time: 99.3 us -> 98.9 us (level)
  no operation moved by 1% of the time
where the time goes in v4:
time: 98.9 us; the launch traced here: 98.8 us
  blocking collectives  37.3 us (38%)
  waiting for transfers between devices  27.3 us (28%)
  starting transfers between devices  15.7 us (16%)
  Pallas kernels  14.7 us (15%)
  local copies, waits for them, and re-layouts  3.03 us (3%)
    all_to_all x1, blocking collectives, shards(): returned = lax.all_to_all(back, ('band', 'lev'), 0, 0, tiled=True)  37.3 us
    all_to_all x1, waiting for transfers between devices, shards(): lax.all_to_all(sent.reshape(256, 8, 128), ('band', 'lev'), 0, 0, tiled=True)  27.3 us
    all_to_all x1, starting transfers between devices, shards(): lax.all_to_all(sent.reshape(256, 8, 128), ('band', 'lev'), 0, 0, tiled=True)  15.7 us
    pallas_call x1, Pallas kernels, shards(): call(head_kernel, 'head', shape((2048, 128), F32), [HBM] * 5, HBM, [pltpu...  6.37 us
    pallas_call x1, Pallas kernels, shards(): call(mid_kernel, 'mid', [shape((256, WAVES), F32), shape((256, 8, 128), F...  4.49 us
    pallas_call x1, Pallas kernels, shards(): call(tail_kernel, 'tail', shape((16, 16, LON), F32), [VMEM] * 4, HBM, [pl...  3.12 us
    unnamed x22, local copies, waits for them, and re-layouts  2.81 us
  transfers between devices with their start and end apart: 1, of which 1 were waited for; matrix products, arithmetic and copies ran while one was open for 0% of the time, Pallas kernels for 1%

profile of v4, /device:TPU:1, one launch (start us, length us, event | category | flops | bytes accessed | tf_op | source)
XLA Modules:
  0.0 98.8 jit_solution(3754160883384313192)
XLA Ops:
  0.6 0.0 copy-start.1
  0.6 0.0 copy-start.2
  0.7 6.4 %head.1 = f32[2048,128]{1,0:T(8,128)} custom-call(s32[1,512]{1,0:T(1,128)} %bitcast.12, f32[256,2048]{1,0:T(8,128)} %bitcast.15, f32[256,2048]{1,0:T(8,128)} %bitcast.16, bf16[2,1024,256]{2,1,0:T(8,128)(2,1)} %constant.21.clone.high_hbm.high_ref, bf16[2,1024,256]{2,1,0:T(8,128)(2,1)} %constant.22.clone.low_hbm.low_ref), custom_call_target="tpu_custom_call" | custom-call | flops 2000000000 | bytes 7000000 | tf_op jit(solution)/shard_map/head/pallas_call | solution.py:321
  7.0 0.0 copy-start.3
  7.0 0.0 copy-start
  7.1 0.0 copy-start.10
  7.1 15.7 %all-to-all-start = ((f32[256,8,128]{2,1,0:T(8,128)}), f32[256,8,128]{2,1,0:T(8,128)S(1)}, u32[]{:S(2)}, u32[]{:S(2)}) async-start(f32[256,8,128]{2,1,0:T(8,128)} %bitcast.14), calls=%async_computation | async-start | bytes 2097152 | tf_op jit(solution)/shard_map/all_to_all | solution.py:327
  22.7 0.0 copy-done.3
  22.7 0.1 dynamic_slice.3
  22.8 0.0 copy-done.1
  22.8 0.0 copy-done.2
  22.8 0.0 copy-done
  22.8 0.7 prepare.1
  23.5 0.0 copy-start.4
  23.6 1.0 copy-done.4
  24.5 0.0 copy-start.5
  24.5 1.0 %copy-done.5 = bf16[2,512,512]{2,1,0:T(8,128)(2,1)} copy-done((bf16[2,512,512]{2,1,0:T(8,128)(2,1)}, bf16[2,512,512]{2,1,0:T(8,128)(2,1)S(1)}, u32[]{:S(2)}) %copy-start.5) | copy-done | bytes 1048600
  25.5 0.0 copy-start.6
  25.5 0.8 copy-done.6
  26.3 27.3 %all-to-all-done.y_ref = f32[256,8,128]{2,1,0:T(8,128)S(1)} async-done(((f32[256,8,128]{2,1,0:T(8,128)}), f32[256,8,128]{2,1,0:T(8,128)S(1)}, u32[]{:S(2)}, u32[]{:S(2)}) %all-to-all-start) | async-done | bytes 1048608 | tf_op jit(solution)/shard_map/all_to_all | solution.py:327
  53.7 0.1 broadcast_in_dim.4.waves_ref
  53.7 0.0 copy-done.10
  53.7 0.1 broadcast_in_dim.5.rates_ref
  53.8 0.0 copy-start.9
  53.8 4.5 %mid.1 = (f32[256,512]{1,0:T(8,128)}, f32[256,8,128]{2,1,0:T(8,128)S(1)}) custom-call(s32[2,512]{1,0:T(2,128)S(1)} %broadcast_in_dim.4.waves_ref, f32[64,128]{1,0:T(8,128)S(1)} %broadcast_in_dim.5.rates_ref, bf16[2,64,192]{2,1,0:T(8,128)(2,1)S(1)} %get-tuple-element.8.couple_ref, f32[256,8,128]{2,1,0:T(8,128)S(1)} %all-to-all-done.y_ref, ...), custom_call_target="tpu_custom_call" | custom-call | flops 3000000000 | bytes 8000000 | tf_op jit(solution)/shard_map/mid/pallas_call | solution.py:339
  58.3 0.0 copy-start.7
  58.3 0.0 copy-start.8
  58.3 37.3 %all_to_all.10 = f32[256,8,128]{2,1,0:T(8,128)S(1)} all-to-all(f32[256,8,128]{2,1,0:T(8,128)S(1)} %get-tuple-element.12), channel_id=1, replica_groups=mesh['band'=64,'lev'=4] {'band','lev'}, dimensions={0} | all-to-all | bytes 2097152 | tf_op jit(solution)/shard_map/all_to_all | solution.py:346
  95.6 0.0 copy-done.9
  95.6 0.0 copy-done.7
  95.6 0.0 copy-done.8
  95.7 3.1 %tail.1 = f32[16,16,2048]{2,1,0:T(8,128)} custom-call(f32[2048,128]{1,0:T(8,128)S(1)} %bitcast.11, bf16[512,512]{1,0:T(8,128)(2,1)S(1)} %copy-done.7, bf16[2,1024,256]{2,1,0:T(8,128)(2,1)S(1)} %copy-done.9, bf16[2,1024,256]{2,1,0:T(8,128)(2,1)S(1)} %copy-done.8), custom_call_target="tpu_custom_call" | custom-call | flops 2000000000 | bytes 6000000 | tf_op jit(solution)/shard_map/tail/pallas_call | solution.py:347
Async XLA Ops:
  0.6 22.2 %copy-start.1 = (f32[64,64]{1,0:T(8,128)S(1)}, f32[64,64]{1,0:T(8,128)}, u32[]{:S(2)}) copy-start(f32[64,64]{1,0:T(8,128)} %to_ref.1) | copy-start | bytes 49156
  0.6 22.2 %copy-start.2 = (f32[64,64]{1,0:T(8,128)S(1)}, f32[64,64]{1,0:T(8,128)}, u32[]{:S(2)}) copy-start(f32[64,64]{1,0:T(8,128)} %from_ref.1) | copy-start | bytes 49156
  7.0 15.7 %copy-start.3 = (s32[512]{0:T(512)S(1)}, s32[512]{0:T(512)}, u32[]{:S(2)}) copy-start(s32[512]{0:T(512)} %param.13) | copy-start | bytes 6148
  7.0 15.8 %copy-start = (f32[2,512,512]{2,1,0:T(8,128)S(1)}, f32[2,512,512]{2,1,0:T(8,128)}, u32[]{:S(2)}) copy-start(f32[2,512,512]{2,1,0:T(8,128)} %p_ref.1) | copy-start | bytes 6291460
  7.1 46.7 %copy-start.10 = (f32[64]{0:T(128)S(1)}, f32[64]{0:T(128)}, u32[]{:S(2)}) copy-start(f32[64]{0:T(128)} %param.17) | copy-start | bytes 772
  7.1 46.6 %all-to-all-start = ((f32[256,8,128]{2,1,0:T(8,128)}), f32[256,8,128]{2,1,0:T(8,128)S(1)}, u32[]{:S(2)}, u32[]{:S(2)}) async-start(f32[256,8,128]{2,1,0:T(8,128)} %bitcast.14), calls=%async_computation | async-start | bytes 2097152 | tf_op jit(solution)/shard_map/all_to_all | solution.py:327
  23.5 1.0 copy-start.4
  24.5 1.0 %copy-start.5 = (bf16[2,512,512]{2,1,0:T(8,128)(2,1)}, bf16[2,512,512]{2,1,0:T(8,128)(2,1)S(1)}, u32[]{:S(2)}) copy-start(bf16[2,512,512]{2,1,0:T(8,128)(2,1)S(1)} %get-tuple-element.10.pl_hbm) | copy-start | bytes 3145732
  25.5 0.8 copy-start.6
  53.8 41.8 %copy-start.9 = (bf16[2,1024,256]{2,1,0:T(8,128)(2,1)S(1)}, bf16[2,1024,256]{2,1,0:T(8,128)(2,1)}, u32[]{:S(2)}) copy-start(bf16[2,1024,256]{2,1,0:T(8,128)(2,1)} %constant.21.clone.high_hbm.high_ref) | copy-start | bytes 3145732
  58.3 37.3 %copy-start.7 = (bf16[512,512]{1,0:T(8,128)(2,1)S(1)}, bf16[512,512]{1,0:T(8,128)(2,1)}, u32[]{:S(2)}) copy-start(bf16[512,512]{1,0:T(8,128)(2,1)} %copy-done.6) | copy-start | bytes 1572868
  58.3 37.3 %copy-start.8 = (bf16[2,1024,256]{2,1,0:T(8,128)(2,1)S(1)}, bf16[2,1024,256]{2,1,0:T(8,128)(2,1)}, u32[]{:S(2)}) copy-start(bf16[2,1024,256]{2,1,0:T(8,128)(2,1)} %constant.22.clone.low_hbm.low_ref) | copy-start | bytes 3145732

commit v5 on v4

--- a/solution.py
+++ b/solution.py
@@ -44,7 +44,7 @@
 
 
 def mm3(a, b):
-    return mm(a[0], b[0]) + (mm(a[0], b[1]) + mm(a[1], b[0]))
+    return mm(jnp.concatenate([a[0], a[0], a[1]], axis=1), jnp.concatenate([b[0], b[1], b[0]], axis=0))
 
 
 def mm3_nt(a, b):

time: 98.9 us -> 98.9 us (level)
  no operation moved by 1% of the time
where the time goes in v5:
time: 98.9 us; the launch traced here: 98.8 us
  blocking collectives  37.3 us (38%)
  waiting for transfers between devices  27.3 us (28%)
  starting transfers between devices  15.7 us (16%)
  Pallas kernels  14.7 us (15%)
  local copies, waits for them, and re-layouts  3.03 us (3%)
    all_to_all x1, blocking collectives, shards(): returned = lax.all_to_all(back, ('band', 'lev'), 0, 0, tiled=True)  37.3 us
    all_to_all x1, waiting for transfers between devices, shards(): lax.all_to_all(sent.reshape(256, 8, 128), ('band', 'lev'), 0, 0, tiled=True)  27.3 us
    all_to_all x1, starting transfers between devices, shards(): lax.all_to_all(sent.reshape(256, 8, 128), ('band', 'lev'), 0, 0, tiled=True)  15.7 us
    pallas_call x1, Pallas kernels, shards(): call(head_kernel, 'head', shape((2048, 128), F32), [HBM] * 5, HBM, [pltpu...  6.37 us
    pallas_call x1, Pallas kernels, shards(): call(mid_kernel, 'mid', [shape((256, WAVES), F32), shape((256, 8, 128), F...  4.48 us
    pallas_call x1, Pallas kernels, shards(): call(tail_kernel, 'tail', shape((16, 16, LON), F32), [VMEM] * 4, HBM, [pl...  3.11 us
    unnamed x22, local copies, waits for them, and re-layouts  2.81 us
  transfers between devices with their start and end apart: 1, of which 1 were waited for; matrix products, arithmetic and copies ran while one was open for 0% of the time, Pallas kernels for 1%

profile of v5, /device:TPU:1, one launch (start us, length us, event | category | flops | bytes accessed | tf_op | source)
XLA Modules:
  0.0 98.8 jit_solution(8395993521146027991)
XLA Ops:
  0.6 0.0 copy-start.1
  0.6 0.0 copy-start.2
  0.7 6.4 %head.1 = f32[2048,128]{1,0:T(8,128)} custom-call(s32[1,512]{1,0:T(1,128)} %bitcast.12, f32[256,2048]{1,0:T(8,128)} %bitcast.15, f32[256,2048]{1,0:T(8,128)} %bitcast.16, bf16[2,1024,256]{2,1,0:T(8,128)(2,1)} %constant.21.clone.high_hbm.high_ref, bf16[2,1024,256]{2,1,0:T(8,128)(2,1)} %constant.22.clone.low_hbm.low_ref), custom_call_target="tpu_custom_call" | custom-call | flops 2000000000 | bytes 7000000 | tf_op jit(solution)/shard_map/head/pallas_call | solution.py:321
  7.0 0.0 copy-start.3
  7.0 0.0 copy-start
  7.1 0.0 copy-start.10
  7.1 15.7 %all-to-all-start = ((f32[256,8,128]{2,1,0:T(8,128)}), f32[256,8,128]{2,1,0:T(8,128)S(1)}, u32[]{:S(2)}, u32[]{:S(2)}) async-start(f32[256,8,128]{2,1,0:T(8,128)} %bitcast.14), calls=%async_computation | async-start | bytes 2097152 | tf_op jit(solution)/shard_map/all_to_all | solution.py:327
  22.7 0.0 copy-done.3
  22.7 0.1 dynamic_slice.3
  22.8 0.0 copy-done.1
  22.8 0.0 copy-done.2
  22.8 0.0 copy-done
  22.8 0.7 prepare.1
  23.5 0.0 copy-start.4
  23.6 1.0 copy-done.4
  24.5 0.0 copy-start.5
  24.5 1.0 %copy-done.5 = bf16[2,512,512]{2,1,0:T(8,128)(2,1)} copy-done((bf16[2,512,512]{2,1,0:T(8,128)(2,1)}, bf16[2,512,512]{2,1,0:T(8,128)(2,1)S(1)}, u32[]{:S(2)}) %copy-start.5) | copy-done | bytes 1048600
  25.5 0.0 copy-start.6
  25.5 0.8 copy-done.6
  26.3 27.3 %all-to-all-done.y_ref = f32[256,8,128]{2,1,0:T(8,128)S(1)} async-done(((f32[256,8,128]{2,1,0:T(8,128)}), f32[256,8,128]{2,1,0:T(8,128)S(1)}, u32[]{:S(2)}, u32[]{:S(2)}) %all-to-all-start) | async-done | bytes 1048608 | tf_op jit(solution)/shard_map/all_to_all | solution.py:327
  53.7 0.1 broadcast_in_dim.4.waves_ref
  53.7 0.0 copy-done.10
  53.7 0.1 broadcast_in_dim.5.rates_ref
  53.8 0.0 copy-start.9
  53.8 4.5 %mid.1 = (f32[256,512]{1,0:T(8,128)}, f32[256,8,128]{2,1,0:T(8,128)S(1)}) custom-call(s32[2,512]{1,0:T(2,128)S(1)} %broadcast_in_dim.4.waves_ref, f32[64,128]{1,0:T(8,128)S(1)} %broadcast_in_dim.5.rates_ref, bf16[2,64,192]{2,1,0:T(8,128)(2,1)S(1)} %get-tuple-element.8.couple_ref, f32[256,8,128]{2,1,0:T(8,128)S(1)} %all-to-all-done.y_ref, ...), custom_call_target="tpu_custom_call" | custom-call | flops 3000000000 | bytes 8000000 | tf_op jit(solution)/shard_map/mid/pallas_call | solution.py:339
  58.3 0.0 copy-start.7
  58.3 0.0 copy-start.8
  58.3 37.3 %all_to_all.10 = f32[256,8,128]{2,1,0:T(8,128)S(1)} all-to-all(f32[256,8,128]{2,1,0:T(8,128)S(1)} %get-tuple-element.12), channel_id=1, replica_groups=mesh['band'=64,'lev'=4] {'band','lev'}, dimensions={0} | all-to-all | bytes 2097152 | tf_op jit(solution)/shard_map/all_to_all | solution.py:346
  95.6 0.0 copy-done.9
  95.6 0.0 copy-done.7
  95.6 0.0 copy-done.8
  95.6 3.1 %tail.1 = f32[16,16,2048]{2,1,0:T(8,128)} custom-call(f32[2048,128]{1,0:T(8,128)S(1)} %bitcast.11, bf16[512,512]{1,0:T(8,128)(2,1)S(1)} %copy-done.7, bf16[2,1024,256]{2,1,0:T(8,128)(2,1)S(1)} %copy-done.9, bf16[2,1024,256]{2,1,0:T(8,128)(2,1)S(1)} %copy-done.8), custom_call_target="tpu_custom_call" | custom-call | flops 2000000000 | bytes 6000000 | tf_op jit(solution)/shard_map/tail/pallas_call | solution.py:347
Async XLA Ops:
  0.6 22.2 %copy-start.1 = (f32[64,64]{1,0:T(8,128)S(1)}, f32[64,64]{1,0:T(8,128)}, u32[]{:S(2)}) copy-start(f32[64,64]{1,0:T(8,128)} %to_ref.1) | copy-start | bytes 49156
  0.6 22.2 %copy-start.2 = (f32[64,64]{1,0:T(8,128)S(1)}, f32[64,64]{1,0:T(8,128)}, u32[]{:S(2)}) copy-start(f32[64,64]{1,0:T(8,128)} %from_ref.1) | copy-start | bytes 49156
  7.0 15.7 %copy-start.3 = (s32[512]{0:T(512)S(1)}, s32[512]{0:T(512)}, u32[]{:S(2)}) copy-start(s32[512]{0:T(512)} %param.13) | copy-start | bytes 6148
  7.0 15.8 %copy-start = (f32[2,512,512]{2,1,0:T(8,128)S(1)}, f32[2,512,512]{2,1,0:T(8,128)}, u32[]{:S(2)}) copy-start(f32[2,512,512]{2,1,0:T(8,128)} %p_ref.1) | copy-start | bytes 6291460
  7.1 46.7 %copy-start.10 = (f32[64]{0:T(128)S(1)}, f32[64]{0:T(128)}, u32[]{:S(2)}) copy-start(f32[64]{0:T(128)} %param.17) | copy-start | bytes 772
  7.1 46.6 %all-to-all-start = ((f32[256,8,128]{2,1,0:T(8,128)}), f32[256,8,128]{2,1,0:T(8,128)S(1)}, u32[]{:S(2)}, u32[]{:S(2)}) async-start(f32[256,8,128]{2,1,0:T(8,128)} %bitcast.14), calls=%async_computation | async-start | bytes 2097152 | tf_op jit(solution)/shard_map/all_to_all | solution.py:327
  23.5 1.0 copy-start.4
  24.5 1.0 %copy-start.5 = (bf16[2,512,512]{2,1,0:T(8,128)(2,1)}, bf16[2,512,512]{2,1,0:T(8,128)(2,1)S(1)}, u32[]{:S(2)}) copy-start(bf16[2,512,512]{2,1,0:T(8,128)(2,1)S(1)} %get-tuple-element.10.pl_hbm) | copy-start | bytes 3145732
  25.5 0.8 copy-start.6
  53.8 41.8 %copy-start.9 = (bf16[2,1024,256]{2,1,0:T(8,128)(2,1)S(1)}, bf16[2,1024,256]{2,1,0:T(8,128)(2,1)}, u32[]{:S(2)}) copy-start(bf16[2,1024,256]{2,1,0:T(8,128)(2,1)} %constant.21.clone.high_hbm.high_ref) | copy-start | bytes 3145732
  58.3 37.3 %copy-start.7 = (bf16[512,512]{1,0:T(8,128)(2,1)S(1)}, bf16[512,512]{1,0:T(8,128)(2,1)}, u32[]{:S(2)}) copy-start(bf16[512,512]{1,0:T(8,128)(2,1)} %copy-done.6) | copy-start | bytes 1572868
  58.3 37.3 %copy-start.8 = (bf16[2,1024,256]{2,1,0:T(8,128)(2,1)S(1)}, bf16[2,1024,256]{2,1,0:T(8,128)(2,1)}, u32[]{:S(2)}) copy-start(bf16[2,1024,256]{2,1,0:T(8,128)(2,1)} %constant.22.clone.low_hbm.low_ref) | copy-start | bytes 3145732
